TPU v7x, 32 devices: a whole 2x2x4 slice. The times are simulated.
32 devices in a mesh: dp: 8 (over y, x, core), head: 4 (over z).
Axes of the slice: x: 2, y: 2, z: 4, core: 2. Of those that a mesh axis runs over, the one named last changes fastest.
Arguments:
- latents: bfloat16 [12288, 1024], P('dp'), may hold values from -6 to 6
- media_tokens: bfloat16 [49152, 1024], P('dp'), may hold values from -6 to 6
- image_counts: int32 [64], replicated, may hold values from 1 to 5, 192 in all
- time_table: bfloat16 [5, 1024], replicated, may hold values from -3 to 3
- media_gain: float32 [1024], replicated, may hold values from 0.5 to 1.5
- media_bias: float32 [1024], replicated, may hold values from -1 to 1
- latent_gain: float32 [1024], replicated, may hold values from 0.5 to 1.5
- latent_bias: float32 [1024], replicated, may hold values from -1 to 1
- feed_gain: float32 [1024], replicated, may hold values from 0.5 to 1.5
- feed_bias: float32 [1024], replicated, may hold values from -1 to 1
- query_weight: bfloat16 [1024, 512], P('dp', 'head'), may hold values from -0.1875 to 0.1875
- key_weight: bfloat16 [1024, 512], P('dp', 'head'), may hold values from -0.1875 to 0.1875
- value_weight: bfloat16 [1024, 512], P('dp', 'head'), may hold values from -0.1875 to 0.1875
- out_weight: bfloat16 [512, 1024], P('head', 'dp'), may hold values from -1 to 1
- up_weight: bfloat16 [1024, 4096], P('dp', 'head'), may hold values from -0.1875 to 0.1875
- down_weight: bfloat16 [4096, 1024], P('head', 'dp'), may hold values from -0.09375 to 0.09375
- cotangent: bfloat16 [12288, 1024], P('dp', 'head'), may hold values from -6 to 6
Outputs:
- latents_out: float32 [12288, 1024], P('dp', 'head')
- latents_grad: float32 [12288, 1024], P('dp')
- time_grad: float32 [5, 1024], replicated
- media_gain_grad: float32 [1024], replicated
- media_bias_grad: float32 [1024], replicated
- latent_gain_grad: float32 [1024], replicated
- latent_bias_grad: float32 [1024], replicated
- feed_gain_grad: float32 [1024], replicated
- feed_bias_grad: float32 [1024], replicated
- query_grad: float32 [1024, 512], P('dp', 'head')
- key_grad: float32 [1024, 512], P('dp', 'head')
- value_grad: float32 [1024, 512], P('dp', 'head')
- out_grad: float32 [512, 1024], P('head', 'dp')
- up_grad: float32 [1024, 4096], P('dp', 'head')
- down_grad: float32 [4096, 1024], P('head', 'dp')
Inputs may be any that keep to these rules, and one draw needn't show every extreme that they name: `image_counts`: each sample holds 1 to 5 images, the counts sum to 192, and some sample holds exactly 5.
All inputs are finite; a program needn't handle non-finite values.
Results may differ from a plain program's by a relative error of at most 0.017.
Values may be sent and summed in bfloat16 or wider, within the bound.
No kernel may reach another device: no remote copies, remote signals or barrier semaphores. Data moves between devices by JAX's collectives and lax.ppermute only.
A program may use at most 192 MiB of HBM per device.

v0:
```python
import math

import jax
import jax.numpy as jnp
from jax import lax
from jax.sharding import PartitionSpec as P

D = 1024
DH = 64
LAT = 64
PATCH = 256
MAX_MEDIA = 5
IMG_DEV = 24


epsilon = 1e-05
highest = lax.Precision.HIGHEST


def contract_rows(left, right):
    return lax.dot_general(
        left, right, (((0,), (0,)), ((), ())), preferred_element_type=jnp.float32
    )


def contract_cols(left, right):
    return lax.dot_general(
        left, right, (((1,), (1,)), ((), ())), preferred_element_type=jnp.float32
    )


def norm_stats(values_in):
    centre = jnp.mean(values_in, axis=-1, keepdims=True)
    shifted = values_in - centre
    spread = jnp.mean(shifted * shifted, axis=-1, keepdims=True)
    inverse = lax.rsqrt(spread + epsilon)
    return (shifted * inverse, inverse)


def norm_back(grad_in, scaled, inverse, norm_gain):
    weighted = grad_in * norm_gain
    return inverse * (
        weighted
        - jnp.mean(weighted, axis=-1, keepdims=True)
        - scaled * jnp.mean(weighted * scaled, axis=-1, keepdims=True)
    )


def gelu_exact(up_proj):
    return up_proj * 0.5 * (1.0 + lax.erf(up_proj * 0.5**0.5))


def gelu_slope(up_proj):
    normal_cdf = 0.5 * (1.0 + lax.erf(up_proj * 0.5**0.5))
    normal_pdf = jnp.exp(-0.5 * up_proj * up_proj) * (2.0 * math.pi) ** (-0.5)
    return normal_cdf + up_proj * normal_pdf


def per_device(
    latents,
    media_tokens,
    image_counts,
    time_table,
    media_gain,
    media_bias,
    latent_gain,
    latent_bias,
    feed_gain,
    feed_bias,
    query_weight,
    key_weight,
    value_weight,
    out_weight,
    up_weight,
    down_weight,
    cotangent,
):
    full_weights = (
        lax.all_gather(query_weight, "dp", axis=0, tiled=True),
        lax.all_gather(key_weight, "dp", axis=0, tiled=True),
        lax.all_gather(value_weight, "dp", axis=0, tiled=True),
        lax.all_gather(out_weight, "dp", axis=1, tiled=True),
        lax.all_gather(up_weight, "dp", axis=0, tiled=True),
        lax.all_gather(down_weight, "dp", axis=1, tiled=True),
    )
    query_full, key_full, value_full, out_full, up_full, down_full = full_weights
    local_width = query_full.shape[1]
    head_size = DH
    heads_here = local_width // head_size
    score_scale = head_size ** (-0.5)
    key_rows = PATCH + LAT
    lat_rows = IMG_DEV * LAT
    block_images = math.gcd(IMG_DEV, 8)
    blocks = IMG_DEV // block_images
    first_image = lax.axis_index("dp") * IMG_DEV
    counts_sum = jnp.cumsum(image_counts)
    starts = counts_sum - image_counts
    image_index = first_image + jnp.arange(IMG_DEV, dtype=jnp.int32)
    latest = jnp.max(jnp.where(starts[None, :] <= image_index[:, None], starts[None, :], 0), axis=1)
    media_slots = image_index - latest
    slot_match = media_slots[:, None] == jnp.arange(MAX_MEDIA, dtype=jnp.int32)[None, :]
    per_image = jnp.dot(
        slot_match.astype(jnp.bfloat16), time_table, preferred_element_type=jnp.float32
    )
    media_sum = media_tokens.reshape(IMG_DEV, PATCH, D).astype(jnp.float32) + per_image[:, None, :]
    media_scaled, media_inverse = norm_stats(media_sum)
    media_norm = (
        (media_scaled * media_gain + media_bias).astype(jnp.bfloat16).reshape(IMG_DEV * PATCH, D)
    )
    latent_scaled, latent_inverse = norm_stats(latents.astype(jnp.float32))
    latent_norm = (latent_scaled * latent_gain + latent_bias).astype(jnp.bfloat16)
    kv_weight = jnp.concatenate([key_full, value_full], axis=1)
    query = jnp.dot(latent_norm, query_full, preferred_element_type=jnp.float32).astype(
        jnp.bfloat16
    )
    media_kv = jnp.dot(media_norm, kv_weight, preferred_element_type=jnp.float32).astype(
        jnp.bfloat16
    )
    latent_kv = jnp.dot(latent_norm, kv_weight, preferred_element_type=jnp.float32).astype(
        jnp.bfloat16
    )
    kv_all = jnp.concatenate(
        [
            media_kv.reshape(IMG_DEV, PATCH, 2 * local_width),
            latent_kv.reshape(IMG_DEV, LAT, 2 * local_width),
        ],
        axis=1,
    )

    def split_heads(query_block, kv_block):
        query_heads = query_block.reshape(block_images, LAT, heads_here, head_size)
        key_heads = kv_block[:, :, :local_width].reshape(
            block_images, key_rows, heads_here, head_size
        )
        value_heads = kv_block[:, :, local_width:].reshape(
            block_images, key_rows, heads_here, head_size
        )
        return (query_heads, key_heads, value_heads)

    def attend_forward(parts):
        query_heads, key_heads, value_heads = split_heads(parts[0], parts[1])
        scores = (
            jnp.einsum(
                "bqhe,bkhe->bhqk", query_heads, key_heads, preferred_element_type=jnp.float32
            )
            * score_scale
        )
        row_top = jnp.max(scores, axis=-1, keepdims=True)
        expd = jnp.exp(scores - row_top)
        row_total = jnp.sum(expd, axis=-1, keepdims=True)
        probability = (expd / row_total).astype(jnp.bfloat16)
        mixed_heads = jnp.einsum(
            "bhqk,bkhe->bqhe", probability, value_heads, preferred_element_type=jnp.float32
        )
        log_total = (row_top + jnp.log(row_total))[..., 0]
        return (mixed_heads.astype(jnp.bfloat16).reshape(block_images, LAT, local_width), log_total)

    query_blocks = query.reshape(blocks, block_images, LAT, local_width)
    kv_blocks = kv_all.reshape(blocks, block_images, key_rows, 2 * local_width)
    mixed_blocks, log_totals = lax.map(attend_forward, (query_blocks, kv_blocks))
    mixed = mixed_blocks.reshape(lat_rows, local_width)
    attention = lax.psum(
        jnp.dot(mixed, out_full, preferred_element_type=jnp.float32).astype(jnp.bfloat16), "head"
    ).astype(jnp.float32)
    hidden = latents.astype(jnp.float32) + attention
    feed_scaled, feed_inverse = norm_stats(hidden)
    feed_norm = (feed_scaled * feed_gain + feed_bias).astype(jnp.bfloat16)
    up_proj = jnp.dot(feed_norm, up_full, preferred_element_type=jnp.float32)
    activation = gelu_exact(up_proj).astype(jnp.bfloat16)
    down_term = jnp.dot(activation, down_full, preferred_element_type=jnp.float32)
    down_share = lax.psum_scatter(
        down_term.astype(jnp.bfloat16), "head", scatter_dimension=1, tiled=True
    ).astype(jnp.float32)
    share_cols = down_share.shape[1]
    hidden_share = lax.dynamic_slice_in_dim(
        hidden, lax.axis_index("head") * share_cols, share_cols, 1
    )
    latents_out = hidden_share + down_share
    back_weights = (
        lax.all_gather(query_weight, "dp", axis=0, tiled=True),
        lax.all_gather(key_weight, "dp", axis=0, tiled=True),
        lax.all_gather(value_weight, "dp", axis=0, tiled=True),
        lax.all_gather(out_weight, "dp", axis=1, tiled=True),
        lax.all_gather(up_weight, "dp", axis=0, tiled=True),
        lax.all_gather(down_weight, "dp", axis=1, tiled=True),
    )
    query_back, key_back, value_back, out_back, up_back, down_back = back_weights
    kv_back = jnp.concatenate([key_back, value_back], axis=1)
    grad_out = lax.all_gather(cotangent, "head", axis=1, tiled=True)
    d_act = contract_cols(grad_out, down_back)
    d_up = (d_act * gelu_slope(up_proj)).astype(jnp.bfloat16)
    down_local = contract_rows(activation, grad_out)
    up_local = contract_rows(feed_norm, d_up)
    mlp_shares = (up_local, down_local)
    feed_term = contract_cols(d_up, up_back)
    feed_gain_part = jnp.sum(feed_term * feed_scaled, axis=0)
    feed_bias_part = jnp.sum(feed_term, axis=0)
    d_feed = lax.psum(feed_term.astype(jnp.bfloat16), "head").astype(jnp.float32)
    d_hidden = grad_out.astype(jnp.float32) + norm_back(
        d_feed, feed_scaled, feed_inverse, feed_gain
    )
    d_attention = d_hidden.astype(jnp.bfloat16)
    out_local = contract_rows(mixed, d_attention)
    d_mixed = contract_cols(d_attention, out_back).astype(jnp.bfloat16)

    def attend_backward(parts):
        query_heads, key_heads, value_heads = split_heads(parts[0], parts[1])
        scores = (
            jnp.einsum(
                "bqhe,bkhe->bhqk", query_heads, key_heads, preferred_element_type=jnp.float32
            )
            * score_scale
        )
        soft_exact = jnp.exp(scores - parts[2][..., None])
        probability = soft_exact.astype(jnp.bfloat16)
        mixed_grad = parts[3].reshape(block_images, LAT, heads_here, head_size)
        d_prob = jnp.einsum(
            "bqhe,bkhe->bhqk", mixed_grad, value_heads, preferred_element_type=jnp.float32
        )
        d_value = jnp.einsum(
            "bhqk,bqhe->bkhe", probability, mixed_grad, preferred_element_type=jnp.float32
        )
        row_delta = jnp.sum(soft_exact * d_prob, axis=-1, keepdims=True)
        d_scores = (soft_exact * (d_prob - row_delta)).astype(jnp.bfloat16)
        d_query = (
            jnp.einsum("bhqk,bkhe->bqhe", d_scores, key_heads, preferred_element_type=jnp.float32)
            * score_scale
        )
        d_key = (
            jnp.einsum("bhqk,bqhe->bkhe", d_scores, query_heads, preferred_element_type=jnp.float32)
            * score_scale
        )
        d_kv = jnp.concatenate(
            [
                d_key.astype(jnp.bfloat16).reshape(block_images, key_rows, local_width),
                d_value.astype(jnp.bfloat16).reshape(block_images, key_rows, local_width),
            ],
            axis=-1,
        )
        return (d_query.astype(jnp.bfloat16).reshape(block_images, LAT, local_width), d_kv)

    mixed_grad_blocks = d_mixed.reshape(blocks, block_images, LAT, local_width)
    d_query_blocks, d_kv_blocks = lax.map(
        attend_backward, (query_blocks, kv_blocks, log_totals, mixed_grad_blocks)
    )
    d_query = d_query_blocks.reshape(lat_rows, local_width)
    d_kv_all = d_kv_blocks.reshape(IMG_DEV, key_rows, 2 * local_width)
    d_media_kv = d_kv_all[:, :PATCH].reshape(IMG_DEV * PATCH, 2 * local_width)
    d_latent_kv = d_kv_all[:, PATCH:].reshape(lat_rows, 2 * local_width)
    query_local = contract_rows(latent_norm, d_query)
    kv_local = contract_rows(media_norm, d_media_kv) + contract_rows(latent_norm, d_latent_kv)
    all_shares = (
        lax.psum_scatter(query_local, "dp", scatter_dimension=0, tiled=True),
        lax.psum_scatter(kv_local[:, :local_width], "dp", scatter_dimension=0, tiled=True),
        lax.psum_scatter(kv_local[:, local_width:], "dp", scatter_dimension=0, tiled=True),
        lax.psum_scatter(out_local, "dp", scatter_dimension=1, tiled=True),
        lax.psum_scatter(mlp_shares[0], "dp", scatter_dimension=0, tiled=True),
        lax.psum_scatter(mlp_shares[1], "dp", scatter_dimension=1, tiled=True),
    )
    query_share, key_share, value_share, out_share, up_share, down_share_grad = all_shares
    latent_term = contract_cols(d_query, query_back) + contract_cols(d_latent_kv, kv_back)
    media_term = contract_cols(d_media_kv, kv_back).reshape(IMG_DEV, PATCH, D)
    latent_gain_part = jnp.sum(latent_term * latent_scaled, axis=0)
    latent_bias_part = jnp.sum(latent_term, axis=0)
    media_gain_part = jnp.sum(media_term * media_scaled, axis=(0, 1))
    media_bias_part = jnp.sum(media_term, axis=(0, 1))
    media_back = norm_back(media_term, media_scaled, media_inverse, media_gain)
    image_sums = jnp.sum(media_back, axis=1)
    time_part = jnp.dot(slot_match.astype(jnp.float32).T, image_sums, precision=highest)
    d_latent_norm = lax.psum(latent_term.astype(jnp.bfloat16), "head").astype(jnp.float32)
    latents_grad = d_hidden + norm_back(d_latent_norm, latent_scaled, latent_inverse, latent_gain)
    small_sums = lax.psum(
        (
            time_part,
            media_gain_part,
            media_bias_part,
            latent_gain_part,
            latent_bias_part,
            feed_gain_part,
            feed_bias_part,
        ),
        ("dp", "head"),
    )
    return (
        latents_out,
        latents_grad,
        small_sums[0],
        small_sums[1],
        small_sums[2],
        small_sums[3],
        small_sums[4],
        small_sums[5],
        small_sums[6],
        query_share,
        key_share,
        value_share,
        out_share,
        up_share,
        down_share_grad,
    )


def solution(mesh):
    return jax.shard_map(
        per_device,
        mesh=mesh,
        in_specs=(
            P("dp", None),
            P("dp", None),
            P(),
            P(),
            P(),
            P(),
            P(),
            P(),
            P(),
            P(),
            P("dp", "head"),
            P("dp", "head"),
            P("dp", "head"),
            P("head", "dp"),
            P("dp", "head"),
            P("head", "dp"),
            P("dp", "head"),
        ),
        out_specs=(
            P("dp", "head"),
            P("dp", None),
            P(),
            P(),
            P(),
            P(),
            P(),
            P(),
            P(),
            P("dp", "head"),
            P("dp", "head"),
            P("dp", "head"),
            P("head", "dp"),
            P("dp", "head"),
            P("head", "dp"),
        ),
        check_vma=False,
    )
```

profile of v0, /device:TPU:0, one launch (start us, length us, event | category | flops | bytes accessed | tf_op | source)
XLA Modules:
  0.0 781.9 jit_solution(15719514503636823679)
XLA Ops:
  10.5 2.9 fusion.22
  14.4 7.1 fusion.5
  21.7 8.4 %multiply_reduce_fusion.4 = f32[6144]{0:T(1024)S(1)} fusion(bf16[6144,1024]{1,0:T(8,128)(2,1)} %param.22, f32[6144]{0:T(1024)S(1)} %broadcast_multiply_fusion.2, f32[24,1024]{1,0:T(8,128)S(1)} %fusion.45), kind=kLoop, calls=%fused_computation.32 | loop fusion | flops 31451136 | bytes 12730368 | tf_op jit(solution)/shard_map/reduce_sum | solution.py:35
  30.2 10.8 %all_gather.29 = bf16[1024,128]{1,0:T(8,128)(2,1)S(1)} all-gather(bf16[128,128]{1,0:T(8,128)(2,1)S(1)} %copy-done.31), channel_id=1, replica_groups=mesh['dp'=8,'head'=4] {'dp'}, dimensions={0}, use_global_device_ids=true | all-gather | bytes 294912 | tf_op jit(solution)/shard_map/all_gather | solution.py:79
  41.0 10.3 %all_gather.30 = bf16[128,1024]{1,0:T(8,128)(2,1)} all-gather(bf16[128,128]{1,0:T(8,128)(2,1)S(1)} %copy-done.32), channel_id=1, replica_groups=mesh['dp'=8,'head'=4] {'dp'}, dimensions={1}, use_global_device_ids=true | all-gather | bytes 294912 | tf_op jit(solution)/shard_map/all_gather | solution.py:82
  51.3 8.4 %all_gather.27 = bf16[1024,128]{1,0:T(8,128)(2,1)S(1)} all-gather(bf16[128,128]{1,0:T(8,128)(2,1)S(1)} %copy-done.33), channel_id=1, replica_groups=mesh['dp'=8,'head'=4] {'dp'}, dimensions={0}, use_global_device_ids=true | all-gather | bytes 294912 | tf_op jit(solution)/shard_map/all_gather | solution.py:80
  59.7 9.4 %all_gather.28 = bf16[1024,128]{1,0:T(8,128)(2,1)S(1)} all-gather(bf16[128,128]{1,0:T(8,128)(2,1)S(1)} %copy-done.34), channel_id=1, replica_groups=mesh['dp'=8,'head'=4] {'dp'}, dimensions={0}, use_global_device_ids=true | all-gather | bytes 294912 | tf_op jit(solution)/shard_map/all_gather | solution.py:81
  76.9 8.9 %add_convert_fusion.1 = bf16[6144,1024]{1,0:T(8,128)(2,1)S(1)} fusion(bf16[6144,1024]{1,0:T(8,128)(2,1)} %param.22, f32[1024]{0:T(1024)S(1)} %copy-done.39, f32[1024]{0:T(1024)S(1)} %copy-done.26, f32[6144]{0:T(1024)S(1)} %add_rsqrt_fusion, f32[6144]{0:T(1024)S(1)} %broadcast_multiply_fusion.2, f32[24,1024]{1,0:T(8,128)S(1)} %fusion.45), kind=kLoop, calls=%fused_computation.31 | loop fusion | flops 44040192 | bytes 25321472 | tf_op jit(solution)/shard_map/convert_element_type | solution.py:108
  85.9 4.9 convolution_convert_fusion.2
  90.7 4.7 copy.57
  95.4 5.3 pad_maximum_fusion
  101.5 17.9 %while.24 = (s32[]{:T(128)}, bf16[3,8,64,128]{3,2,1,0:T(8,128)(2,1)}, f32[3,8,2,64]{3,2,1,0:T(2,128)}, bf16[3,8,320,256]{2,3,1,0:T(8,128)(2,1)}, bf16[3,8,64,128]{3,2,1,0:T(8,128)(2,1)}, /*index=5*/s32[]{:T(128)}) while((s32[]{:T(128)}, bf16[3,8,64,128]{3,2,1,0:T(8,128)(2,1)}, f32[3,8,2,64]{3,2,1,0:T(2,128)}, ...), condition=%wide.region_9.10_spmd, body=%wide.region_6.9_spmd.sunk | while | flops 86244352 | bytes 11833437 | solution.py:160
  119.4 3.7 convolution_convert_fusion.3
  125.4 153.5 %all-reduce.5.cloned.1.call-done = bf16[1536,1024]{1,0:T(8,128)(2,1)} async-done(((bf16[1536,1024]{1,0:T(8,128)(2,1)}), bf16[1536,1024]{1,0:T(8,128)(2,1)}) %all-reduce.5.cloned.1.call-update) | async-done | bytes 3145744 | tf_op jit(solution)/shard_map/psum | solution.py:162
  278.8 2.9 fusion.49
  283.1 3.0 add_convert_fusion.3
  286.2 8.2 %multiply_convert_fusion.2 = (bf16[1536,1024]{1,0:T(8,128)(2,1)}, f32[1536,1024]{1,0:T(8,128)}) fusion(bf16[1536,1024]{1,0:T(8,128)(2,1)} %add_convert_fusion.3, bf16[1024,1024]{1,0:T(8,128)(2,1)} %all-gather.4.cloned.1.call-done), kind=kOutput, calls=%fused_computation.71 | convolution fusion | flops 3229089792 | bytes 14680064 | tf_op jit(solution)/shard_map/dot_general | solution.py:168
  295.1 8.9 %fusion.28 = bf16[1536,1024]{1,0:T(8,128)(2,1)S(1)} fusion(f32[1536,1024]{1,0:T(8,128)} %get-tuple-element.145, bf16[1536,1024]{1,0:T(8,128)(2,1)} %all-gather.8.cloned.1.call-done, bf16[1024,1024]{1,0:T(8,128)(2,1)} %all-gather.6.cloned.1.call-done), kind=kOutput, calls=%fused_computation.63 | convolution fusion | flops 3236954112 | bytes 14680064 | tf_op jit(solution)/shard_map/dot_general | solution.py:27
  304.1 5.8 fusion.55
  310.0 7.6 convolution_convert_fusion.4
  317.9 112.3 %all-reduce.7.cloned.1.call-done = bf16[1536,1024]{1,0:T(8,128)(2,1)} async-done(((bf16[1536,1024]{1,0:T(8,128)(2,1)}), bf16[1536,1024]{1,0:T(8,128)(2,1)}) %all-reduce.7.cloned.1.call-update) | async-done | bytes 3145744 | tf_op jit(solution)/shard_map/psum | solution.py:198
  430.2 7.3 multiply_reduce_fusion.6
  437.6 4.5 multiply_add_fusion
  442.1 2.6 copy-done.3
  447.2 57.0 %while.25 = (s32[]{:T(128)}, bf16[3,8,64,128]{3,2,1,0:T(8,128)(2,1)}, bf16[3,8,320,256]{3,2,1,0:T(8,128)(2,1)}, bf16[3,8,320,256]{2,3,1,0:T(8,128)(2,1)}, bf16[3...) while((s32[]{:T(128)}, ...), condition=%wide.region_19.20_spmd, body=%wide.region_17.19_spmd.sunk | while | flops 216071168 | bytes 28987532 | solution.py:243
  457.9 2.7 maximum_bitcast_fusion.2
  460.6 2.5 copy.87
  476.9 2.7 maximum_bitcast_fusion.2
  479.6 2.5 copy.87
  482.8 2.5 constant_dynamic-update-slice_fusion.10
  495.9 2.7 maximum_bitcast_fusion.2
  498.6 2.5 copy.87
  508.5 4.6 fusion.56
  513.2 4.2 fusion.34
  519.2 3.8 fusion.59
  523.0 4.1 fusion.60
  527.2 23.0 %multiply_reduce_fusion.5 = (f32[24,256]{1,0:T(8,128)S(1)}, f32[24,256]{1,0:T(8,128)S(1)}, f32[24,256,1024]{2,1,0:T(8,128)}, f32[24,256,1024]{2,1,0:T(8,128)}) fusion(f32[1024]{0:T(1024)S(1)} %copy-done.27, f32[24,256]{1,0:T(8,128)S(1)} %rsqrt.31, f32[24,256]{1,0:T(8,128)S(1)} %div.57, f32[24,1024]{1,0:T(8,128)S(1)} %copy-done.11, ...), kind=kOutput, calls=%fused_computation.35 | convolution fusion | flops 3271544832 | bytes 66785280 | tf_op jit(solution)/shard_map/dot_general | solution.py:27
  550.2 11.9 %fusion.40 = f32[1024,256]{1,0:T(8,128)S(1)} fusion(f32[1024,256]{1,0:T(8,128)S(1)} %copy-done.46, bf16[24,320,256]{2,1,0:T(8,128)(2,1)} %bitcast.174, f32[1024]{0:T(1024)S(1)} %copy-done.40, f32[1024]{0:T(1024)S(1)} %copy-done.27, f32[24,256]{1,0:T(8,128)S(1)} %rsqrt.31, f32[24,256]{1,0:T(8,128)S(1)} %div.57, f32[24,256,1024]{2,1,0:T(8,128)} %get-tuple-element.129, ...), kind=kOutput, calls=%fused_computation.91 | convolution fusion | flops 3259236352 | bytes 30564352 | tf_op jit(solution)/shard_map/dot_general | solution.py:21
  564.0 8.4 %fusion.62 = f32[1024,1024]{1,0:T(8,128)} fusion(bf16[1536,1024]{1,0:T(8,128)(2,1)} %get-tuple-element.144, bf16[1536,1024]{1,0:T(8,128)(2,1)} %all-gather.8.cloned.1.call-done), kind=kOutput, calls=%fused_computation.128 | convolution fusion | flops 3221225472 | bytes 10485760 | tf_op jit(solution)/shard_map/dot_general | solution.py:21
  572.7 8.4 %fusion.61 = f32[1024,1024]{1,0:T(8,128)} fusion(bf16[1536,1024]{1,0:T(8,128)(2,1)} %add_convert_fusion.3, bf16[1536,1024]{1,0:T(8,128)(2,1)} %copy-done.45), kind=kOutput, calls=%fused_computation.127 | convolution fusion | flops 3221225472 | bytes 10485760 | tf_op jit(solution)/shard_map/dot_general | solution.py:21
  581.2 19.2 %multiply_reduce_fusion.1 = (f32[1024]{0:T(1024)S(1)}, f32[24,1024]{1,0:T(8,128)S(1)}, f32[1024]{0:T(1024)S(1)}) fusion(f32[24,256,1024]{2,1,0:T(8,128)} %get-tuple-element.150, f32[24,256]{1,0:T(8,128)S(1)} %rsqrt.31, f32[24,256]{1,0:T(8,128)S(1)} %div.57, f32[24,256,1024]{2,1,0:T(8,128)} %get-tuple-element.129, f32[24,1024]{1,0:T(8,128)S(1)} %copy-done.11, ...), kind=kLoop, calls=%fused_computation.27 | loop fusion | flops 75470848 | bytes 50638848 | tf_op jit(solution)/shard_map/reduce_sum | solution.py:265
  600.8 3.0 convert_add_fusion.1
  603.8 29.3 %all-reduce.9.cloned.1.call-done = bf16[1536,1024]{1,0:T(8,128)(2,1)} async-done(((bf16[1536,1024]{1,0:T(8,128)(2,1)}), bf16[1536,1024]{1,0:T(8,128)(2,1)}) %all-reduce.9.cloned.1.call-update) | async-done | bytes 3145744 | tf_op jit(solution)/shard_map/psum | solution.py:270
  633.2 5.8 fusion.50
  638.9 40.5 %all-reduce = (f32[5,1024]{1,0:T(8,128)}, f32[1024]{0:T(1024)}, f32[1024]{0:T(1024)}, f32[1024]{0:T(1024)}, f32[1024]{0:T(1024)}, /*index=5*/f32[1024]{0:T(1024)}, f32[1024]{0:T(1024)}) all-reduce(f32[5,1024]{1,0:T(8,128)S(1)} %fusion.44, f32[1024]{0:T(1024)S(1)} %get-tuple-element.85, ...), channel_id=1, replica_groups=mesh['dp'=8,'head'=4] {'dp','head'}, use_global_device_ids=true, to_apply=%region_26.27 | all-reduce | flops 11264 | bytes 90112 | tf_op jit(solution)/shard_map/psum | solution.py:272
  679.4 6.9 fusion.20
  686.4 32.6 %reduce-scatter.20.cloned.1.call-done = f32[1024,128]{1,0:T(8,128)} async-done(((f32[1024,1024]{1,0:T(8,128)}), f32[1024,128]{1,0:T(8,128)}) %reduce-scatter.20.cloned.1.call-update) | async-done | bytes 524304 | tf_op jit(solution)/shard_map/reduce_scatter | solution.py:258
  719.0 55.1 %reduce-scatter.18.cloned.1.call-done = f32[128,1024]{1,0:T(8,128)} async-done(((f32[1024,1024]{1,0:T(8,128)}), f32[128,1024]{1,0:T(8,128)}) %reduce-scatter.18.cloned.1.call-update) | async-done | bytes 524304 | tf_op jit(solution)/shard_map/reduce_scatter | solution.py:257
  (243 shorter events, 84.5 us)
Async XLA Ops:
  8.0 5.9 copy-start
  8.0 270.8 %all-reduce.5.cloned.1.call-start = ((), (), s32[]{:S(2)}) async-start(), calls=%async_computation.7 | async-start | bytes 6291456 | tf_op jit(solution)/shard_map/psum | solution.py:162
  10.5 58.7 %copy-start.22 = (f32[1536]{0:T(1024)}, f32[1536]{0:T(1024)S(1)}, u32[]{:S(2)}) copy-start(f32[1536]{0:T(1024)S(1)} %broadcast_multiply_fusion.8) | copy-start | bytes 18436
  13.4 55.8 %copy-start.24 = (f32[1536]{0:T(1024)}, f32[1536]{0:T(1024)S(1)}, u32[]{:S(2)}) copy-start(f32[1536]{0:T(1024)S(1)} %add_rsqrt_fusion.2) | copy-start | bytes 18436
  14.4 62.4 %copy-start.10 = (f32[24,1024]{1,0:T(8,128)}, f32[24,1024]{1,0:T(8,128)S(1)}, u32[]{:S(2)}) copy-start(f32[24,1024]{1,0:T(8,128)S(1)} %fusion.45) | copy-start | bytes 294916
  21.6 55.3 %copy-start.20 = (f32[6144]{0:T(1024)}, f32[6144]{0:T(1024)S(1)}, u32[]{:S(2)}) copy-start(f32[6144]{0:T(1024)S(1)} %broadcast_multiply_fusion.2) | copy-start | bytes 73732
  21.6 8.5 %copy-start.31 = (bf16[128,128]{1,0:T(8,128)(2,1)S(1)}, bf16[128,128]{1,0:T(8,128)(2,1)}, u32[]{:S(2)}) copy-start(bf16[128,128]{1,0:T(8,128)(2,1)} %param.31) | copy-start | bytes 98308
  21.6 19.3 %copy-start.32 = (bf16[128,128]{1,0:T(8,128)(2,1)S(1)}, bf16[128,128]{1,0:T(8,128)(2,1)}, u32[]{:S(2)}) copy-start(bf16[128,128]{1,0:T(8,128)(2,1)} %param.34) | copy-start | bytes 98308
  21.6 29.6 %copy-start.33 = (bf16[128,128]{1,0:T(8,128)(2,1)S(1)}, bf16[128,128]{1,0:T(8,128)(2,1)}, u32[]{:S(2)}) copy-start(bf16[128,128]{1,0:T(8,128)(2,1)} %param.32) | copy-start | bytes 98308
  21.6 38.1 %copy-start.34 = (bf16[128,128]{1,0:T(8,128)(2,1)S(1)}, bf16[128,128]{1,0:T(8,128)(2,1)}, u32[]{:S(2)}) copy-start(bf16[128,128]{1,0:T(8,128)(2,1)} %param.33) | copy-start | bytes 98308
  21.7 47.6 %copy-start.2 = (bf16[1536,1024]{1,0:T(8,128)(2,1)S(1)}, bf16[1536,1024]{1,0:T(8,128)(2,1)}, u32[]{:S(2)}) copy-start(bf16[1536,1024]{1,0:T(8,128)(2,1)} %param.21) | copy-start | bytes 9437188
  21.7 47.6 %copy-start.28 = (f32[1024]{0:T(1024)S(1)}, f32[1024]{0:T(1024)}, u32[]{:S(2)}) copy-start(f32[1024]{0:T(1024)} %param.27) | copy-start | bytes 12292
  21.7 47.6 %copy-start.37 = (f32[1024]{0:T(1024)S(1)}, f32[1024]{0:T(1024)}, u32[]{:S(2)}) copy-start(f32[1024]{0:T(1024)} %param.28) | copy-start | bytes 12292
  30.2 46.7 %copy-start.21 = (f32[6144]{0:T(1024)}, f32[6144]{0:T(1024)S(1)}, u32[]{:S(2)}) copy-start(f32[6144]{0:T(1024)S(1)} %add_rsqrt_fusion) | copy-start | bytes 73732
  41.0 31.6 %copy-start.18 = (bf16[1024,128]{1,0:T(8,128)(2,1)}, bf16[1024,128]{1,0:T(8,128)(2,1)S(1)}, u32[]{:S(2)}) copy-start(bf16[1024,128]{1,0:T(8,128)(2,1)S(1)} %all_gather.29) | copy-start | bytes 786436
  70.7 6.1 copy-start.26
  70.8 6.1 copy-start.39
  76.9 8.9 %copy-start.15 = (bf16[1024,256]{1,0:T(8,128)(2,1)S(1)}, bf16[1024,256]{1,0:T(8,128)(2,1)}, u32[]{:S(2)}) copy-start(bf16[1024,256]{1,0:T(8,128)(2,1)} %copy-done.14) | copy-start | bytes 1572868
  123.1 163.0 %all-gather.4.cloned.1.call-start = ((), (), s32[]{:S(2)}) async-start(), calls=%async_computation.8 | async-start | bytes 2359296 | tf_op jit(solution)/shard_map/all_gather | solution.py:83
  123.7 170.6 %all-gather.6.cloned.1.call-start = ((), (), s32[]{:S(2)}) async-start(), calls=%async_computation.9 | async-start | bytes 2359296 | tf_op jit(solution)/shard_map/all_gather | solution.py:84
  124.3 170.8 %all-gather.8.cloned.1.call-start = ((), (), s32[]{:S(2)}) async-start(), calls=%async_computation.11 | async-start | bytes 3932160 | tf_op jit(solution)/shard_map/all_gather | solution.py:189
  124.9 158.2 %copy-start.30 = (f32[1024]{0:T(1024)S(1)}, f32[1024]{0:T(1024)}, u32[]{:S(2)}) copy-start(f32[1024]{0:T(1024)} %param.29) | copy-start | bytes 12292
  124.9 158.2 %copy-start.38 = (f32[1024]{0:T(1024)S(1)}, f32[1024]{0:T(1024)}, u32[]{:S(2)}) copy-start(f32[1024]{0:T(1024)} %param.30) | copy-start | bytes 12292
  124.9 305.2 %all-reduce.7.cloned.1.call-start = ((), (), s32[]{:S(2)}) async-start(), calls=%async_computation.12 | async-start | bytes 6291456 | tf_op jit(solution)/shard_map/psum | solution.py:198
  295.1 8.9 %copy-start.44 = (bf16[1024,1024]{1,0:T(8,128)(2,1)S(1)}, bf16[1024,1024]{1,0:T(8,128)(2,1)}, u32[]{:S(2)}) copy-start(bf16[1024,1024]{1,0:T(8,128)(2,1)} %all-gather.4.cloned.1.call-done) | copy-start | bytes 6291460
  304.1 5.9 copy-start.45
  309.9 290.8 %reduce-scatter.8.cloned.1.call-start = ((), (), s32[]{:S(2)}) async-start(), calls=%async_computation.10 | async-start | bytes 3932160 | tf_op jit(solution)/shard_map/reduce_scatter | solution.py:171
  317.6 315.5 %all-reduce.9.cloned.1.call-start = ((), (), s32[]{:S(2)}) async-start(), calls=%async_computation.13 | async-start | bytes 6291456 | tf_op jit(solution)/shard_map/psum | solution.py:270
  430.1 7.3 copy-start.5
  430.1 7.3 copy-start.8
  430.1 7.5 copy-start.16
  437.6 7.1 copy-start.17
  513.1 173.2 %reduce-scatter.16.cloned.1.call-start = ((), (), s32[]{:S(2)}) async-start(), calls=%async_computation.17 | async-start | bytes 589824 | tf_op jit(solution)/shard_map/reduce_scatter | solution.py:256
  517.4 168.9 %reduce-scatter.10.cloned.1.call-start = ((), (), s32[]{:S(2)}) async-start(), calls=%async_computation.14 | async-start | bytes 589824 | tf_op jit(solution)/shard_map/reduce_scatter | solution.py:253
  519.2 8.0 %copy-start.11 = (f32[24,1024]{1,0:T(8,128)S(1)}, f32[24,1024]{1,0:T(8,128)}, u32[]{:S(2)}) copy-start(f32[24,1024]{1,0:T(8,128)} %copy-done.10) | copy-start | bytes 294916
  519.2 8.0 %copy-start.27 = (f32[1024]{0:T(1024)S(1)}, f32[1024]{0:T(1024)}, u32[]{:S(2)}) copy-start(f32[1024]{0:T(1024)} %param.25) | copy-start | bytes 12292
  527.1 159.2 %reduce-scatter.14.cloned.1.call-start = ((), (), s32[]{:S(2)}) async-start(), calls=%async_computation.16 | async-start | bytes 589824 | tf_op jit(solution)/shard_map/reduce_scatter | solution.py:255
  527.2 23.0 %copy-start.40 = (f32[1024]{0:T(1024)S(1)}, f32[1024]{0:T(1024)}, u32[]{:S(2)}) copy-start(f32[1024]{0:T(1024)} %param.26) | copy-start | bytes 12292
  527.2 23.0 %copy-start.46 = (f32[1024,256]{1,0:T(8,128)S(1)}, f32[1024,256]{1,0:T(8,128)}, u32[]{:S(2)}) copy-start(f32[1024,256]{1,0:T(8,128)} %fusion.60) | copy-start | bytes 3145732
  563.3 123.1 %reduce-scatter.12.cloned.1.call-start = ((), (), s32[]{:S(2)}) async-start(), calls=%async_computation.15 | async-start | bytes 589824 | tf_op jit(solution)/shard_map/reduce_scatter | solution.py:254
  564.0 155.0 %reduce-scatter.20.cloned.1.call-start = ((), (), s32[]{:S(2)}) async-start(), calls=%async_computation.19 | async-start | bytes 4718592 | tf_op jit(solution)/shard_map/reduce_scatter | solution.py:258
  572.4 201.6 %reduce-scatter.18.cloned.1.call-start = ((), (), s32[]{:S(2)}) async-start(), calls=%async_computation.18 | async-start | bytes 4718592 | tf_op jit(solution)/shard_map/reduce_scatter | solution.py:257
  581.2 19.3 %copy-start.42 = (s32[24]{0:T(128)S(1)}, s32[24]{0:T(128)}, u32[]{:S(2)}) copy-start(s32[24]{0:T(128)} %copy-done.41) | copy-start | bytes 292
  581.2 51.9 %copy-start.23 = (f32[1536]{0:T(1024)S(1)}, f32[1536]{0:T(1024)}, u32[]{:S(2)}) copy-start(f32[1536]{0:T(1024)} %copy-done.22) | copy-start | bytes 18436
  581.2 51.9 %copy-start.25 = (f32[1536]{0:T(1024)S(1)}, f32[1536]{0:T(1024)}, u32[]{:S(2)}) copy-start(f32[1536]{0:T(1024)} %copy-done.24) | copy-start | bytes 18436
  581.2 51.9 %copy-start.29 = (f32[1024]{0:T(1024)S(1)}, f32[1024]{0:T(1024)}, u32[]{:S(2)}) copy-start(f32[1024]{0:T(1024)} %param.27) | copy-start | bytes 12292
  633.1 5.8 copy-start.36
  679.4 94.6 %copy-start.1 = (bf16[5,1024]{1,0:T(8,128)(2,1)S(1)}, bf16[5,1024]{1,0:T(8,128)(2,1)}, u32[]{:S(2)}) copy-start(bf16[5,1024]{1,0:T(8,128)(2,1)} %param.24) | copy-start | bytes 30724
  (14 other events, 43.7 us)
Sparse Core Ops, SparseCore 0:
  123.3 155.5 all-reduce.4
  310.1 120.0 all-reduce.6
  432.5 59.4 reduce-scatter.7
  517.5 33.1 reduce-scatter.15
  554.2 34.1 reduce-scatter.9
  591.9 34.1 reduce-scatter.13
  629.7 34.2 reduce-scatter.11
  667.9 51.0 reduce-scatter.19
  722.9 51.1 reduce-scatter.17
Sparse Core Ops, SparseCore 1:
  125.5 27.9 all-gather.3
  155.2 27.9 all-gather.5
  184.6 110.4 all-gather.7
  513.2 119.9 all-reduce.8
where the time goes:
time: 789 us; the launch traced here: 782 us
  waiting for transfers between devices  386 us (49%)
  matrix products  133 us (17%)
  other arithmetic  103 us (13%)
  blocking collectives  79.4 us (10%)
  local copies, waits for them, and re-layouts  61.8 us (8%)
  between operations  16.7 us (2%)
    psum x1, waiting for transfers between devices, per_device(): lax.psum(jnp.dot(mixed, out_full, preferred_element_type=jnp.float32).ast...  153 us
    psum x1, waiting for transfers between devices, per_device(): lax.psum(feed_term.astype(jnp.bfloat16), 'head').astype(jnp.float32)  112 us
    reduce_scatter x1, waiting for transfers between devices, per_device(): lax.psum_scatter(mlp_shares[0], 'dp', scatter_dimension=0, tiled=True)  55.1 us
    dot_general x6, matrix products, contract_cols(): lax.dot_general(left, right, (((1,), (1,)), ((), ())), preferred_element_...  46.1 us
    dot_general x6, matrix products, contract_rows(): lax.dot_general(left, right, (((0,), (0,)), ((), ())), preferred_element_...  40.8 us
    psum x1, blocking collectives, per_device(): lax.psum((time_part, media_gain_part, media_bias_part, latent_gain_part,...  40.5 us
    reduce_scatter x1, waiting for transfers between devices, per_device(): lax.psum_scatter(mlp_shares[1], 'dp', scatter_dimension=1, tiled=True)  32.6 us
    psum x1, waiting for transfers between devices, per_device(): lax.psum(latent_term.astype(jnp.bfloat16), 'head').astype(jnp.float32)  29.3 us
  transfers between devices with their start and end apart: 13, of which 6 were waited for; matrix products, arithmetic and copies ran while one was open for 26% of the time, Pallas kernels for 0%

commit v1 on v0

v1 whole, which is shorter than its diff:
```python
import math

import jax
import jax.numpy as jnp
from jax import lax
from jax.experimental import pallas as pl
from jax.experimental.pallas import tpu as pltpu
from jax.sharding import PartitionSpec as P

D = 1024
DH = 64
LAT = 64
PATCH = 256
MAX_MEDIA = 5
GROUP = 4

epsilon = 1e-05
highest = lax.Precision.HIGHEST
bf16 = jnp.bfloat16
f32 = jnp.float32


def mm(left, right):
    return lax.dot_general(left, right, (((1,), (0,)), ((), ())), preferred_element_type=f32)


def mm_tn(left, right):
    return lax.dot_general(left, right, (((0,), (0,)), ((), ())), preferred_element_type=f32)


def mm_nt(left, right):
    return lax.dot_general(left, right, (((1,), (1,)), ((), ())), preferred_element_type=f32)


def norm_stats(values_in):
    centre = jnp.mean(values_in, axis=-1, keepdims=True)
    shifted = values_in - centre
    spread = jnp.mean(shifted * shifted, axis=-1, keepdims=True)
    inverse = lax.rsqrt(spread + epsilon)
    return (shifted * inverse, inverse)


def norm_back(grad_in, scaled, inverse, norm_gain):
    weighted = grad_in * norm_gain
    return inverse * (
        weighted
        - jnp.mean(weighted, axis=-1, keepdims=True)
        - scaled * jnp.mean(weighted * scaled, axis=-1, keepdims=True)
    )


def gelu_exact(up_proj):
    return up_proj * 0.5 * (1.0 + lax.erf(up_proj * 0.5**0.5))


def gelu_slope(up_proj):
    normal_cdf = 0.5 * (1.0 + lax.erf(up_proj * 0.5**0.5))
    normal_pdf = jnp.exp(-0.5 * up_proj * up_proj) * (2.0 * math.pi) ** (-0.5)
    return normal_cdf + up_proj * normal_pdf


def own_blocks():
    width = GROUP * DH
    rows = lax.broadcasted_iota(jnp.int32, (GROUP * LAT, width), 0) // LAT
    cols = lax.broadcasted_iota(jnp.int32, (GROUP * LAT, width), 1) // DH
    return rows == cols


def spread_heads(block, mask):
    return jnp.where(mask, jnp.concatenate([block] * GROUP, axis=0), jnp.zeros((), block.dtype))


def gather_heads(blocks, mask):
    kept = jnp.where(mask, blocks, 0.0)
    return sum(kept[g * LAT : (g + 1) * LAT] for g in range(GROUP))


def soft_of(query_diag, keys):
    scores = mm_nt(query_diag, keys) * (DH**-0.5)
    expd = jnp.exp(scores - jnp.max(scores, axis=-1, keepdims=True))
    return expd / jnp.sum(expd, axis=-1, keepdims=True)


def attend_kernel(q_ref, km_ref, kl_ref, vm_ref, vl_ref, mixed_ref):
    mask = own_blocks()
    width = GROUP * DH
    for g in range(q_ref.shape[1] // width):
        cols = slice(g * width, (g + 1) * width)
        keys = jnp.concatenate([km_ref[:, cols], kl_ref[:, cols]], axis=0)
        values = jnp.concatenate([vm_ref[:, cols], vl_ref[:, cols]], axis=0)
        soft = soft_of(spread_heads(q_ref[:, cols], mask), keys)
        mixed_ref[:, cols] = gather_heads(mm(soft.astype(bf16), values), mask).astype(bf16)


def attend_back_kernel(
    q_ref, km_ref, kl_ref, vm_ref, vl_ref, dm_ref, dq_ref, dkm_ref, dkl_ref, dvm_ref, dvl_ref
):
    mask = own_blocks()
    width = GROUP * DH
    for g in range(q_ref.shape[1] // width):
        cols = slice(g * width, (g + 1) * width)
        keys = jnp.concatenate([km_ref[:, cols], kl_ref[:, cols]], axis=0)
        values = jnp.concatenate([vm_ref[:, cols], vl_ref[:, cols]], axis=0)
        query_diag = spread_heads(q_ref[:, cols], mask)
        mixed_diag = spread_heads(dm_ref[:, cols], mask)
        soft = soft_of(query_diag, keys)
        d_prob = mm_nt(mixed_diag, values)
        d_value = mm_tn(soft.astype(bf16), mixed_diag).astype(bf16)
        delta = jnp.sum(soft * d_prob, axis=-1, keepdims=True)
        d_scores = (soft * (d_prob - delta)).astype(bf16)
        d_query = gather_heads(mm(d_scores, keys), mask) * (DH**-0.5)
        d_key = (mm_tn(d_scores, query_diag) * (DH**-0.5)).astype(bf16)
        dq_ref[:, cols] = d_query.astype(bf16)
        dkm_ref[:, cols] = d_key[:PATCH]
        dkl_ref[:, cols] = d_key[PATCH:]
        dvm_ref[:, cols] = d_value[:PATCH]
        dvl_ref[:, cols] = d_value[PATCH:]


def image_spec(rows, cols, block_col=0):
    return pl.BlockSpec((rows, cols), lambda n: (n, block_col))


def attend(query, media_kv, latent_kv):
    inner = query.shape[1]
    images = query.shape[0] // LAT
    return pl.pallas_call(
        attend_kernel,
        grid=(images,),
        in_specs=[
            image_spec(LAT, inner),
            image_spec(PATCH, inner, 0),
            image_spec(LAT, inner, 0),
            image_spec(PATCH, inner, 1),
            image_spec(LAT, inner, 1),
        ],
        out_specs=image_spec(LAT, inner),
        out_shape=jax.ShapeDtypeStruct(query.shape, bf16),
        name="attend",
    )(query, media_kv, latent_kv, media_kv, latent_kv)


def attend_back(query, media_kv, latent_kv, d_mixed):
    inner = query.shape[1]
    images = query.shape[0] // LAT
    media_shape = jax.ShapeDtypeStruct((media_kv.shape[0], inner), bf16)
    latent_shape = jax.ShapeDtypeStruct(query.shape, bf16)
    return pl.pallas_call(
        attend_back_kernel,
        grid=(images,),
        in_specs=[
            image_spec(LAT, inner),
            image_spec(PATCH, inner, 0),
            image_spec(LAT, inner, 0),
            image_spec(PATCH, inner, 1),
            image_spec(LAT, inner, 1),
            image_spec(LAT, inner),
        ],
        out_specs=[
            image_spec(LAT, inner),
            image_spec(PATCH, inner),
            image_spec(LAT, inner),
            image_spec(PATCH, inner),
            image_spec(LAT, inner),
        ],
        out_shape=[latent_shape, media_shape, latent_shape, media_shape, latent_shape],
        name="attend_back",
    )(query, media_kv, latent_kv, media_kv, latent_kv, d_mixed)


def make_step(n_dp, n_head):
    def swap(block, bit):
        return lax.ppermute(block, "dp", [(j, j ^ bit) for j in range(n_dp)])

    def shift(block, step):
        return lax.ppermute(block, "head", [(j, (j + step) % n_head) for j in range(n_head)])

    def swap_head(block, bit):
        return lax.ppermute(block, "head", [(j, j ^ bit) for j in range(n_head)])

    ordered = [1 << b for b in range(1, n_dp.bit_length() - 1)]
    paths = (ordered, ordered[::-1])
    evens = list(range(0, n_dp, 2))
    places = evens + [m | 1 for m in evens]

    def to_own(values_in, me):
        size = D // n_dp
        parts = [lax.dynamic_slice_in_dim(values_in, (me ^ m) * size, size, 1) for m in places]
        return jnp.concatenate(parts, axis=1)

    def to_plain(values_in, me):
        size = D // n_dp
        parts = []
        for j in range(n_dp):
            m = me ^ j
            at = (m >> 1) + (m & 1) * (n_dp // 2)
            parts.append(lax.dynamic_slice_in_dim(values_in, at * size, size, 1))
        return jnp.concatenate(parts, axis=1)

    def gather(shard):
        columns = [shard] + [shift(shard, s) for s in range(1, n_head)]
        half = n_head // 2
        sides = []
        for bits, part in zip(paths, (columns[:half], columns[half:])):
            held = {0: jnp.concatenate(part, axis=1)}
            for bit in bits:
                for m in list(held):
                    held[m | bit] = swap(held[m], bit)
            sides.append(jnp.concatenate([held[m] for m in evens], axis=0))
        even = jnp.concatenate(sides, axis=1)
        return (even, swap(even, 1))

    def scatter(keep, send):
        arrived = swap(send, 1)
        total_rows, total_cols = keep.shape
        rows = total_rows // len(evens)
        half = total_cols // 2
        sides = []
        for bits, side in zip(paths, (0, 1)):
            held = {}
            for at, m in enumerate(evens):
                block = (slice(at * rows, (at + 1) * rows), slice(side * half, (side + 1) * half))
                held[m] = (keep[block].astype(f32) + arrived[block].astype(f32)).astype(bf16)
            for bit in bits[::-1]:
                for m in sorted(held):
                    if m & bit:
                        came = swap(held.pop(m), bit).astype(f32)
                        held[m ^ bit] = (held[m ^ bit].astype(f32) + came).astype(bf16)
            sides.append(held[0])
        width = total_cols // n_head
        per_side = n_head // 2
        total = sides[0][:, :width].astype(f32)
        for s in range(1, n_head):
            at = s % per_side
            piece = sides[s // per_side][:, at * width : (at + 1) * width]
            total = total + shift(piece, n_head - s).astype(f32)
        return total

    def sum_everywhere(values_in):
        for bit in [1 << b for b in range(n_dp.bit_length() - 1)]:
            values_in = values_in + swap(values_in, bit)
        for bit in [1 << b for b in range(n_head.bit_length() - 1)]:
            values_in = values_in + swap_head(values_in, bit)
        return values_in

    def per_device(
        latents,
        media_tokens,
        image_counts,
        time_table,
        media_gain,
        media_bias,
        latent_gain,
        latent_bias,
        feed_gain,
        feed_bias,
        query_weight,
        key_weight,
        value_weight,
        out_weight,
        up_weight,
        down_weight,
        cotangent,
    ):
        me = lax.axis_index("dp")
        my_head = lax.axis_index("head")
        images_dp = latents.shape[0] // LAT
        images = images_dp // n_head
        lat_rows = images * LAT
        media_rows = images * PATCH
        half_d = D // 2

        attention_shard = jnp.concatenate(
            [query_weight, key_weight, value_weight, out_weight.T], axis=1
        )
        width = query_weight.shape[1]
        inner = width * n_head
        attention_even, attention_odd = gather(attention_shard)

        cot_cols = cotangent.shape[1]
        full_cot = jnp.zeros((lat_rows, D), bf16)
        for s in range(n_head):
            target = (my_head + s) % n_head
            block = lax.dynamic_slice_in_dim(cotangent, target * lat_rows, lat_rows, 0)
            if s:
                block = shift(block, s)
            source = (my_head - s) % n_head
            full_cot = lax.dynamic_update_slice_in_dim(full_cot, block, source * cot_cols, 1)
        grad_out = to_own(full_cot, me)

        up_even, up_odd = gather(up_weight)
        down_even, down_odd = gather(down_weight.T)

        first_image = me * images_dp + my_head * images
        counts_sum = jnp.cumsum(image_counts)
        starts = counts_sum - image_counts
        image_index = first_image + jnp.arange(images, dtype=jnp.int32)
        latest = jnp.max(
            jnp.where(starts[None, :] <= image_index[:, None], starts[None, :], 0), axis=1
        )
        media_slots = image_index - latest
        slot_match = media_slots[:, None] == jnp.arange(MAX_MEDIA, dtype=jnp.int32)[None, :]
        vectors = jnp.stack(
            [media_gain, media_bias, latent_gain, latent_bias, feed_gain, feed_bias]
        )
        vectors = to_own(vectors, me)
        media_g, media_b, latent_g, latent_b, feed_g, feed_b = [vectors[j : j + 1] for j in range(6)]
        per_image = jnp.dot(
            slot_match.astype(bf16), to_own(time_table, me), preferred_element_type=f32
        )
        media_own = to_own(
            lax.dynamic_slice_in_dim(media_tokens, my_head * media_rows, media_rows, 0), me
        )
        latents_own = to_own(
            lax.dynamic_slice_in_dim(latents, my_head * lat_rows, lat_rows, 0), me
        ).astype(f32)

        media_sum = (
            media_own.reshape(images, PATCH, D).astype(f32) + per_image[:, None, :]
        ).reshape(media_rows, D)
        media_scaled, media_inverse = norm_stats(media_sum)
        media_norm = (media_scaled * media_g + media_b).astype(bf16)
        latent_scaled, latent_inverse = norm_stats(latents_own)
        latent_norm = (latent_scaled * latent_g + latent_b).astype(bf16)

        def column_part(block, at):
            split = block.reshape(block.shape[0], n_head, 4, width)
            return split[:, :, at].reshape(block.shape[0], inner)

        attention_full = jnp.concatenate([attention_even, attention_odd], axis=0)
        query_full, key_full, value_full, out_full = [
            column_part(attention_full, at) for at in range(4)
        ]
        kv_full = jnp.concatenate([key_full, value_full], axis=1)

        query = mm(latent_norm, query_full).astype(bf16)
        media_kv = mm(media_norm, kv_full).astype(bf16)
        latent_kv = mm(latent_norm, kv_full).astype(bf16)
        mixed = attend(query, media_kv, latent_kv)
        hidden = latents_own + mm_nt(mixed, out_full)
        feed_scaled, feed_inverse = norm_stats(hidden)
        feed_norm = (feed_scaled * feed_g + feed_b).astype(bf16)

        up_full = jnp.concatenate([up_even, up_odd], axis=0)
        down_full = jnp.concatenate([down_even, down_odd], axis=0)
        up_proj = mm(feed_norm, up_full)
        activation = gelu_exact(up_proj).astype(bf16)
        result = hidden + mm_nt(activation, down_full)

        plain_out = to_plain(result.astype(bf16), me)
        out_cols = D // n_head
        latents_out = jnp.zeros((images_dp * LAT, out_cols), f32)
        for s in range(n_head):
            target = (my_head + s) % n_head
            block = lax.dynamic_slice_in_dim(plain_out, target * out_cols, out_cols, 1)
            if s:
                block = shift(block, s)
            source = (my_head - s) % n_head
            latents_out = lax.dynamic_update_slice_in_dim(
                latents_out, block.astype(f32), source * lat_rows, 0
            )

        d_act = mm(grad_out, down_full)
        d_up = (d_act * gelu_slope(up_proj)).astype(bf16)
        down_grad = scatter(
            mm_tn(grad_out[:, :half_d], activation).astype(bf16),
            mm_tn(grad_out[:, half_d:], activation).astype(bf16),
        )
        up_grad = scatter(
            mm_tn(feed_norm[:, :half_d], d_up).astype(bf16),
            mm_tn(feed_norm[:, half_d:], d_up).astype(bf16),
        )
        d_feed = mm_nt(d_up, up_full)
        feed_gain_part = jnp.sum(d_feed * feed_scaled, axis=0)
        feed_bias_part = jnp.sum(d_feed, axis=0)
        d_hidden = grad_out.astype(f32) + norm_back(d_feed, feed_scaled, feed_inverse, feed_g)
        d_attention = d_hidden.astype(bf16)
        d_mixed = mm(d_attention, out_full).astype(bf16)

        d_query, d_key_m, d_key_l, d_value_m, d_value_l = attend_back(
            query, media_kv, latent_kv, d_mixed
        )
        d_media_kv = jnp.concatenate([d_key_m, d_value_m], axis=1)
        d_latent_kv = jnp.concatenate([d_key_l, d_value_l], axis=1)
        d_latent_norm = mm_nt(d_query, query_full) + mm_nt(d_latent_kv, kv_full)
        latent_gain_part = jnp.sum(d_latent_norm * latent_scaled, axis=0)
        latent_bias_part = jnp.sum(d_latent_norm, axis=0)
        latent_back = d_hidden + norm_back(d_latent_norm, latent_scaled, latent_inverse, latent_g)

        own_grad = to_plain(latent_back.astype(bf16), me)
        latents_grad = jnp.zeros((images_dp * LAT, D), f32)
        rising, falling = own_grad, own_grad
        latents_grad = lax.dynamic_update_slice_in_dim(
            latents_grad, own_grad.astype(f32), my_head * lat_rows, 0
        )
        for s in range(1, n_head):
            rising = lax.ppermute(rising, "head", [(j, j + 1) for j in range(n_head - 1)])
            falling = lax.ppermute(falling, "head", [(j, j - 1) for j in range(1, n_head)])
            below = jnp.maximum(my_head - s, 0)
            above = jnp.minimum(my_head + s, n_head - 1)
            kept = lax.dynamic_slice_in_dim(latents_grad, below * lat_rows, lat_rows, 0)
            latents_grad = lax.dynamic_update_slice_in_dim(
                latents_grad,
                jnp.where(my_head >= s, rising.astype(f32), kept),
                below * lat_rows,
                0,
            )
            kept = lax.dynamic_slice_in_dim(latents_grad, above * lat_rows, lat_rows, 0)
            latents_grad = lax.dynamic_update_slice_in_dim(
                latents_grad,
                jnp.where(my_head + s < n_head, falling.astype(f32), kept),
                above * lat_rows,
                0,
            )

        def attention_grads(cols):
            wide = mm_tn(media_norm[:, cols], d_media_kv) + mm_tn(latent_norm[:, cols], d_latent_kv)
            query_part = mm_tn(latent_norm[:, cols], d_query)
            out_part = mm_tn(d_attention[:, cols], mixed)
            parts = [query_part, wide[:, :inner], wide[:, inner:], out_part]
            split = [p.astype(bf16).reshape(half_d, n_head, 1, width) for p in parts]
            return jnp.concatenate(split, axis=2).reshape(half_d, 4 * inner)

        attention_grad = scatter(
            attention_grads(slice(0, half_d)), attention_grads(slice(half_d, D))
        )
        query_grad, key_grad, value_grad, out_grad = [
            attention_grad[:, at * width : (at + 1) * width] for at in range(4)
        ]

        d_media_norm = mm_nt(d_media_kv, kv_full)
        media_gain_part = jnp.sum(d_media_norm * media_scaled, axis=0)
        media_bias_part = jnp.sum(d_media_norm, axis=0)
        media_back = norm_back(d_media_norm, media_scaled, media_inverse, media_g)
        image_sums = jnp.sum(media_back.reshape(images, PATCH, D), axis=1)
        time_part = jnp.dot(slot_match.astype(f32).T, image_sums, precision=highest)
        small = jnp.concatenate(
            [
                time_part,
                jnp.stack(
                    [
                        media_gain_part,
                        media_bias_part,
                        latent_gain_part,
                        latent_bias_part,
                        feed_gain_part,
                        feed_bias_part,
                    ]
                ),
            ],
            axis=0,
        )
        small = sum_everywhere(to_plain(small, me))
        return (
            latents_out,
            latents_grad,
            small[:MAX_MEDIA],
            small[MAX_MEDIA],
            small[MAX_MEDIA + 1],
            small[MAX_MEDIA + 2],
            small[MAX_MEDIA + 3],
            small[MAX_MEDIA + 4],
            small[MAX_MEDIA + 5],
            query_grad,
            key_grad,
            value_grad,
            out_grad.T,
            up_grad,
            down_grad.T,
        )

    return per_device


def solution(mesh):
    per_device = make_step(mesh.shape["dp"], mesh.shape["head"])
    rows, both, flipped, whole = P("dp", None), P("dp", "head"), P("head", "dp"), P()
    return jax.shard_map(
        per_device,
        mesh=mesh,
        in_specs=(rows, rows)
        + (whole,) * 8
        + (both, both, both, flipped, both, flipped, both),
        out_specs=(both, rows) + (whole,) * 7 + (both, both, both, flipped, both, flipped),
        check_vma=False,
    )
```

time: 789 us -> 638 us (0.81)
  waiting for transfers between devices: 386 us -> 174 us
  starting transfers between devices: 1.58 us -> 108 us
  blocking collectives: 79.4 us -> 0 us
  matrix products: 133 us -> 101 us
  other arithmetic: 103 us -> 131 us
  local copies, waits for them, and re-layouts: 61.8 us -> 88.7 us
  Pallas kernels: 0 us -> 18.9 us
  between operations: 16.7 us -> 3.12 us
    psum x3 -> x0, waiting for transfers between devices: 295 us -> none  [the longest x1 153 us: per_device(): lax.psum(jnp.dot(mixed, out_full, preferred_element_type=jnp.float32).ast...]
    ppermute x0 -> x77, waiting for transfers between devices: none -> 174 us  [the longest x45 106 us: swap(): return lax.ppermute(block, 'dp', [(j, j ^ bit) for j in range(n_dp)])]
    ppermute x0 -> x77, starting transfers between devices: none -> 108 us  [the longest x24 45 us: shift(): lax.ppermute(block, 'head', [(j, (j + step) % n_head) for j in range(n_he...]
    reduce_scatter x7 -> x0, waiting for transfers between devices: 87.7 us -> none  [the longest x1 55.1 us: per_device(): lax.psum_scatter(mlp_shares[0], 'dp', scatter_dimension=0, tiled=True)]
    concatenate x1 -> x9, other arithmetic: 5.26 us -> 57.9 us  [the longest x3 37.4 us: gather(): even = jnp.concatenate(sides, axis=1)]
    unnamed x93 -> x296, local copies, waits for them, and re-layouts: 4.22 us -> 54.6 us
    psum x1 -> x0, blocking collectives: 40.5 us -> none  [per_device(): lax.psum((time_part, media_gain_part, media_bias_part, latent_gain_part,...]
    all_gather x4 -> x0, blocking collectives: 38.9 us -> none  [the longest x1 10.8 us: per_device(): lax.all_gather(query_weight, 'dp', axis=0, tiled=True)]
  transfers between devices with their start and end apart: 13 -> 77, of which waited for: 6 -> 27; matrix products, arithmetic and copies ran while one was open for 26% -> 40% of each run, Pallas kernels for 0% -> 1%
where the time goes in v1:
time: 638 us; the launch traced here: 626 us
  waiting for transfers between devices  174 us (27%)
  other arithmetic  131 us (21%)
  starting transfers between devices  108 us (17%)
  matrix products  101 us (16%)
  local copies, waits for them, and re-layouts  88.7 us (14%)
  Pallas kernels  18.9 us (3%)
    ppermute x45, waiting for transfers between devices, swap(): return lax.ppermute(block, 'dp', [(j, j ^ bit) for j in range(n_dp)])  106 us
    unnamed x296, local copies, waits for them, and re-layouts  54.6 us
    ppermute x24, starting transfers between devices, shift(): lax.ppermute(block, 'head', [(j, (j + step) % n_head) for j in range(n_he...  45 us
    ppermute x45, starting transfers between devices, swap(): return lax.ppermute(block, 'dp', [(j, j ^ bit) for j in range(n_dp)])  44.6 us
    dot_general x6, matrix products, mm(): lax.dot_general(left, right, (((1,), (0,)), ((), ())), preferred_element_...  38.3 us
    concatenate x3, other arithmetic, gather(): even = jnp.concatenate(sides, axis=1)  37.4 us
    dot_general x6, matrix products, mm_nt(): lax.dot_general(left, right, (((1,), (1,)), ((), ())), preferred_element_...  33.5 us
    ppermute x24, waiting for transfers between devices, shift(): lax.ppermute(block, 'head', [(j, (j + step) % n_head) for j in range(n_he...  33.4 us
  transfers between devices with their start and end apart: 77, of which 27 were waited for; matrix products, arithmetic and copies ran while one was open for 40% of the time, Pallas kernels for 1%

profile of v1, /device:TPU:0, one launch (start us, length us, event | category | flops | bytes accessed | tf_op | source)
XLA Modules:
  0.0 626.0 jit_solution(9978629288491978829)
XLA Ops:
  4.7 4.1 collective-permute-start.4
  11.8 2.9 collective-permute-start.15
  73.9 8.0 %collective-permute-done.33 = bf16[384,256]{1,0:T(8,128)(2,1)S(1)} collective-permute-done((bf16[384,256]{1,0:T(8,128)(2,1)S(1)}, bf16[384,256]{1,0:T(8,128)(2,1)S(1)}, u32[]{:S(2)}, u32[]{:S(2)}) %collective-permute-start.33) | collective-permute-done | bytes 196640 | tf_op jit(solution)/shard_map/ppermute | solution.py:176
  82.6 5.1 collective-permute-done.34
  91.0 5.0 collective-permute-start.25
  101.3 3.0 collective-permute-start.20
  107.3 4.2 collective-permute-done.24
  117.7 3.0 collective-permute-done.1
  125.8 18.7 %collective-permute-done.8 = bf16[128,1024]{0,1:T(8,128)(2,1)S(1)} collective-permute-done((bf16[128,1024]{0,1:T(8,128)(2,1)S(1)}, bf16[128,1024]{0,1:T(8,128)(2,1)S(1)}, u32[]{:S(2)}, u32[]{:S(2)}) %collective-permute-start.8) | collective-permute-done | bytes 262176 | tf_op jit(solution)/shard_map/ppermute | solution.py:173
  150.2 5.1 maximum_maximum_fusion.2
  155.4 3.9 collective-permute-done.12
  171.1 6.7 %collective-permute-done.13 = bf16[128,2048]{1,0:T(8,128)(2,1)S(1)} collective-permute-done((bf16[128,2048]{1,0:T(8,128)(2,1)S(1)}, bf16[128,2048]{1,0:T(8,128)(2,1)S(1)}, u32[]{:S(2)}, u32[]{:S(2)}) %collective-permute-start.13) | collective-permute-done | bytes 524320 | tf_op jit(solution)/shard_map/ppermute | solution.py:173
  178.0 16.8 %maximum_maximum_fusion = bf16[512,4096]{1,0:T(8,128)(2,1)} fusion(bf16[128,2048]{1,0:T(8,128)(2,1)S(1)} %collective-permute-done.18, bf16[128,2048]{1,0:T(8,128)(2,1)S(1)} %collective-permute-done.17, bf16[128,2048]{1,0:T(8,128)(2,1)S(1)} %collective-permute-done.16, bf16[128,2048]{1,0:T(8,128)(2,1)S(1)} %constant_dynamic-update-slice_fusion.49, ...), kind=kLoop, calls=%fused_computation.27 | loop fusion | flops 33554432 | bytes 8388608 | tf_op jit(solution)/shard_map/concatenate | solution.py:210
  196.3 15.4 %maximum_maximum_fusion.1 = bf16[512,4096]{0,1:T(8,128)(2,1)} fusion(bf16[128,2048]{0,1:T(8,128)(2,1)S(1)} %collective-permute-done.28, bf16[128,2048]{0,1:T(8,128)(2,1)S(1)} %collective-permute-done.27, bf16[128,2048]{0,1:T(8,128)(2,1)S(1)} %collective-permute-done.26, bf16[128,2048]{0,1:T(8,128)(2,1)S(1)} %constant_dynamic-update-slice_fusion.51, ...), kind=kLoop, calls=%fused_computation.28 | loop fusion | flops 37748736 | bytes 8388608 | tf_op jit(solution)/shard_map/concatenate | solution.py:210
  211.9 9.5 %pad_maximum_fusion.2 = bf16[1024,2048]{0,1:T(8,128)(2,1)S(1)} fusion(bf16[512,2048]{0,1:T(8,128)(2,1)S(1)} %collective-permute-done.9, bf16[128,1024]{0,1:T(8,128)(2,1)S(1)} %collective-permute-done.8, bf16[128,1024]{0,1:T(8,128)(2,1)S(1)} %collective-permute-done.7, bf16[128,1024]{0,1:T(8,128)(2,1)S(1)} %collective-permute-done.6, ...), kind=kLoop, calls=%fused_computation.26 | loop fusion | flops 37748736 | bytes 8388608 | tf_op jit(solution)/shard_map/concatenate | solution.py:330
  225.0 5.9 convolution_convert_fusion.4.km_ref.vm_ref
  232.3 7.3 %attend.1 = bf16[384,512]{1,0:T(8,128)(2,1)} custom-call(bf16[384,512]{1,0:T(8,128)(2,1)} %convolution_convert_fusion.11.q_ref, bf16[1536,1024]{1,0:T(8,128)(2,1)} %convolution_convert_fusion.4.km_ref.vm_ref, bf16[384,1024]{1,0:T(8,128)(2,1)} %convolution_convert_fusion.5.kl_ref.vl_ref, bf16[1536,1024]{1,0:T(8,128)(2,1)} %convolution_convert_fusion.4.km_ref.vm_ref, ...), custom_call_target="tpu_custom_call" | custom-call | tf_op jit(solution)/shard_map/attend/pallas_call | solution.py:127
  242.7 7.4 %pad_maximum_fusion = bf16[1024,4096]{1,0:T(8,128)(2,1)S(1)} fusion(bf16[512,4096]{1,0:T(8,128)(2,1)} %collective-permute-done.19, bf16[128,2048]{1,0:T(8,128)(2,1)S(1)} %copy-done.38, bf16[128,2048]{1,0:T(8,128)(2,1)S(1)} %copy-done.30, bf16[128,2048]{1,0:T(8,128)(2,1)S(1)} %copy-done.32, bf16[128,2048]{1,0:T(8,128)(2,1)S(1)} %copy-done.24, ...), kind=kLoop, calls=%fused_computation.1 | loop fusion | flops 75497472 | bytes 16777216 | tf_op jit(solution)/shard_map/concatenate | solution.py:344
  250.3 5.5 multiply_convert_fusion
  255.9 22.2 %fusion.5 = bf16[384,4096]{1,0:T(8,128)(2,1)S(1)} fusion(f32[384,4096]{1,0:T(8,128)S(1)} %get-tuple-element.171, bf16[384,1024]{1,0:T(8,128)(2,1)S(1)} %copy-done.58, bf16[512,4096]{0,1:T(8,128)(2,1)} %collective-permute-done.29, bf16[128,2048]{0,1:T(8,128)(2,1)S(1)} %copy-done.71, bf16[128,2048]{0,1:T(8,128)(2,1)S(1)} %copy-done.63, ...), kind=kOutput, calls=%fused_computation.8 | convolution fusion | flops 3320840192 | bytes 18612224 | tf_op jit(solution)/shard_map/dot_general | solution.py:24
  278.1 4.5 convolution_convert_fusion.2
  282.6 4.4 convolution_convert_fusion.3
  287.0 4.3 multiply_reduce_fusion.4
  296.5 11.7 %attend_back.1 = (bf16[384,512]{1,0:T(8,128)(2,1)}, bf16[1536,512]{1,0:T(8,128)(2,1)}, bf16[384,512]{1,0:T(8,128)(2,1)}, bf16[1536,512]{1,0:T(8,128)(2,1)}, bf16[384,512]{1,0:T(8,128)(2,1)}) custom-call(bf16[384,512]{1,0:T(8,128)(2,1)} %convolution_convert_fusion.11.q_ref, bf16[1536,1024]{1,0:T(8,128)(2,1)} %convolution_convert_fusion.4.km_ref.vm_ref, ...), custom_call_target="tpu_custom_call" | custom-call | tf_op jit(solution)/shard_map/attend_back/pallas_call | solution.py:148
  319.3 7.7 %multiply_reduce_fusion = (f32[1024]{0:T(1024)S(1)}, f32[1536]{0:T(1024)S(1)}, f32[1536]{0:T(1024)S(1)}, f32[1024]{0:T(1024)S(1)}, f32[1536,1024]{1,0:T(8,128)}) fusion(bf16[1536,1024]{1,0:T(8,128)(2,1)S(1)} %get-tuple-element.100, f32[1536]{0:T(1024)S(1)} %rsqrt.29, f32[1536]{0:T(1024)S(1)} %div.41, f32[6,1024]{1,0:T(8,128)S(1)} %copy-done.60, ...), kind=kOutput, calls=%fused_computation.12 | convolution fusion | flops 3242716160 | bytes 14741504 | tf_op jit(solution)/shard_map/dot_general | solution.py:32
  327.1 4.4 convolution_convert_fusion
  345.4 7.5 %subtract_multiply_fusion = f32[1536,1024]{1,0:T(8,128)} fusion(bf16[1536,1024]{1,0:T(8,128)(2,1)S(1)} %get-tuple-element.100, f32[1536,1024]{1,0:T(8,128)} %get-tuple-element.174, f32[1536]{0:T(1024)S(1)} %broadcast_multiply_fusion, f32[1536]{0:T(1024)S(1)} %broadcast_multiply_fusion.1, f32[1024]{0:T(1024)S(1)} %bitcast.147, f32[1536]{0:T(1024)S(1)} %rsqrt.29, ...), kind=kLoop, calls=%fused_computation.13 | loop fusion | flops 14155776 | bytes 15781888 | tf_op jit(solution)/shard_map/mul | solution.py:45
  352.9 3.5 reduce_sum.183
  356.8 3.5 fusion.22
  364.2 13.5 %add_convert_fusion.3 = bf16[384,1024]{1,0:T(8,128)(2,1)S(1)} fusion(f32[384,1024]{1,0:T(8,128)S(1)} %copy-done.1, bf16[384,4096]{1,0:T(8,128)(2,1)S(1)} %copy-done.8, bf16[512,4096]{0,1:T(8,128)(2,1)} %collective-permute-done.29, bf16[128,2048]{0,1:T(8,128)(2,1)} %copy-done.70, bf16[128,2048]{0,1:T(8,128)(2,1)} %copy-done.62, ...), kind=kOutput, calls=%fused_computation.68 | convolution fusion | flops 3305897984 | bytes 13893632 | tf_op jit(solution)/shard_map/dot_general | solution.py:32
  379.0 6.6 %collective-permute-start.30 = (bf16[384,256]{1,0:T(8,128)(2,1)}, bf16[384,256]{1,0:T(8,128)(2,1)}, u32[]{:S(2)}, u32[]{:S(2)}) collective-permute-start(bf16[384,256]{1,0:T(8,128)(2,1)} %get-tuple-element.145), channel_id=1, source_target_pairs={{0,1},{1,2},{2,3},{3,0},{4,5},{5,6},{6,7},{7,4},{8,9},{9,10},{10,1... | collective-permute-start | bytes 589832 | tf_op jit(solution)/shard_map/ppermute | solution.py:176
  385.6 4.5 convolution_convert_fusion.1
  395.7 3.5 broadcast_in_dim.18
  407.7 3.2 collective-permute-start.36
  415.2 5.0 collective-permute-start.46
  421.9 17.3 %collective-permute-done.46 = f32[11,1024]{1,0:T(8,128)S(1)} collective-permute-done((f32[11,1024]{1,0:T(8,128)S(1)}, f32[11,1024]{1,0:T(8,128)S(1)}, u32[]{:S(2)}, u32[]{:S(2)}) %collective-permute-start.46) | collective-permute-done | bytes 45088 | tf_op jit(solution)/shard_map/ppermute | solution.py:179
  451.3 9.7 %collective-permute-done.38 = bf16[384,1024]{1,0:T(8,128)(2,1)S(1)} collective-permute-done((bf16[384,1024]{1,0:T(8,128)(2,1)S(1)}, bf16[384,1024]{1,0:T(8,128)(2,1)S(1)}, u32[]{:S(2)}, u32[]{:S(2)}) %collective-permute-start.38) | collective-permute-done | bytes 786464 | tf_op jit(solution)/shard_map/ppermute | solution.py:397
  461.0 4.4 collective-permute-start.40
  471.6 3.0 collective-permute-done.49
  490.2 3.7 collective-permute-done.53
  495.5 5.5 collective-permute-done.41
  512.7 9.0 %collective-permute-done.69 = bf16[128,2048]{1,0:T(8,128)(2,1)S(1)} collective-permute-done((bf16[128,2048]{1,0:T(8,128)(2,1)S(1)}, bf16[128,2048]{1,0:T(8,128)(2,1)S(1)}, u32[]{:S(2)}, u32[]{:S(2)}) %collective-permute-start.69) | collective-permute-done | bytes 524320 | tf_op jit(solution)/shard_map/ppermute | solution.py:173
  526.4 17.8 %collective-permute-done.59 = bf16[128,2048]{1,0:T(8,128)(2,1)S(1)} collective-permute-done((bf16[128,2048]{1,0:T(8,128)(2,1)S(1)}, bf16[128,2048]{1,0:T(8,128)(2,1)S(1)}, u32[]{:S(2)}, u32[]{:S(2)}) %collective-permute-start.59) | collective-permute-done | bytes 524320 | tf_op jit(solution)/shard_map/ppermute | solution.py:173
  551.8 7.5 %collective-permute-done.60 = bf16[128,2048]{1,0:T(8,128)(2,1)S(1)} collective-permute-done((bf16[128,2048]{1,0:T(8,128)(2,1)S(1)}, bf16[128,2048]{1,0:T(8,128)(2,1)S(1)}, u32[]{:S(2)}, u32[]{:S(2)}) %collective-permute-start.60) | collective-permute-done | bytes 524320 | tf_op jit(solution)/shard_map/ppermute | solution.py:173
  562.2 8.3 %collective-permute-done.73 = bf16[128,2048]{1,0:T(8,128)(2,1)S(1)} collective-permute-done((bf16[128,2048]{1,0:T(8,128)(2,1)S(1)}, bf16[128,2048]{1,0:T(8,128)(2,1)S(1)}, u32[]{:S(2)}, u32[]{:S(2)}) %collective-permute-start.73) | collective-permute-done | bytes 524320 | tf_op jit(solution)/shard_map/ppermute | solution.py:173
  580.6 10.0 %collective-permute-done.63 = bf16[128,2048]{1,0:T(8,128)(2,1)} collective-permute-done((bf16[128,2048]{1,0:T(8,128)(2,1)}, bf16[128,2048]{1,0:T(8,128)(2,1)}, u32[]{:S(2)}, u32[]{:S(2)}) %collective-permute-start.63) | collective-permute-done | bytes 524320 | tf_op jit(solution)/shard_map/ppermute | solution.py:173
  598.2 5.7 collective-permute-done.64
  606.8 14.0 %collective-permute-done.75 = bf16[128,1024]{1,0:T(8,128)(2,1)S(1)} collective-permute-done((bf16[128,1024]{1,0:T(8,128)(2,1)S(1)}, bf16[128,1024]{1,0:T(8,128)(2,1)S(1)}, u32[]{:S(2)}, u32[]{:S(2)}) %collective-permute-start.75) | collective-permute-done | bytes 262176 | tf_op jit(solution)/shard_map/ppermute | solution.py:176
  (550 shorter events, 259.6 us)
Async XLA Ops:
  4.7 61.8 %collective-permute-start.4 = (bf16[128,512]{0,1:T(8,128)(2,1)}, bf16[128,512]{0,1:T(8,128)(2,1)}, u32[]{:S(2)}, u32[]{:S(2)}) collective-permute-start(bf16[128,512]{0,1:T(8,128)(2,1)} %pad_maximum_fusion.7), channel_id=1, source_target_pairs={{0,2},{1,3},{2,0},{3,1},{4,6},{5,7},{6,4},{7,5},{8,10},{9,11},{10,... | collective-permute-start | bytes 393224 | tf_op jit(solution)/shard_map/ppermute | solution.py:176
  8.8 58.9 %collective-permute-start.5 = (bf16[128,512]{0,1:T(8,128)(2,1)}, bf16[128,512]{0,1:T(8,128)(2,1)}, u32[]{:S(2)}, u32[]{:S(2)}) collective-permute-start(bf16[128,512]{0,1:T(8,128)(2,1)} %pad_maximum_fusion.7), channel_id=1, source_target_pairs={{0,3},{1,0},{2,1},{3,2},{4,7},{5,4},{6,5},{7,6},{8,11},{9,8},{10,9... | collective-permute-start | bytes 393224 | tf_op jit(solution)/shard_map/ppermute | solution.py:176
  10.1 60.2 %collective-permute-start = (bf16[128,512]{0,1:T(8,128)(2,1)}, bf16[128,512]{0,1:T(8,128)(2,1)}, u32[]{:S(2)}, u32[]{:S(2)}) collective-permute-start(bf16[128,512]{0,1:T(8,128)(2,1)} %pad_maximum_fusion.7), channel_id=1, source_target_pairs={{0,1},{1,2},{2,3},{3,0},{4,5},{5,6},{6,7},{7,4},{8,9},{9,10},{10,1... | collective-permute-start | bytes 393224 | tf_op jit(solution)/shard_map/ppermute | solution.py:176
  10.8 90.5 %collective-permute-start.14 = (bf16[128,1024]{1,0:T(8,128)(2,1)}, bf16[128,1024]{1,0:T(8,128)(2,1)}, u32[]{:S(2)}, u32[]{:S(2)}) collective-permute-start(bf16[128,1024]{1,0:T(8,128)(2,1)} %param.31), channel_id=1, source_target_pairs={{0,2},{1,3},{2,0},{3,1},{4,6},{5,7},{6,4},{7,5},{8,10},{9,11},{10,... | collective-permute-start | bytes 786440 | tf_op jit(solution)/shard_map/ppermute | solution.py:176
  11.8 92.5 %collective-permute-start.15 = (bf16[128,1024]{1,0:T(8,128)(2,1)}, bf16[128,1024]{1,0:T(8,128)(2,1)}, u32[]{:S(2)}, u32[]{:S(2)}) collective-permute-start(bf16[128,1024]{1,0:T(8,128)(2,1)} %param.31), channel_id=1, source_target_pairs={{0,3},{1,0},{2,1},{3,2},{4,7},{5,4},{6,5},{7,6},{8,11},{9,8},{10,9... | collective-permute-start | bytes 786440 | tf_op jit(solution)/shard_map/ppermute | solution.py:176
  66.5 39.3 %collective-permute-start.10 = (bf16[128,1024]{1,0:T(8,128)(2,1)S(1)}, bf16[128,1024]{1,0:T(8,128)(2,1)S(1)}, u32[]{:S(2)}, u32[]{:S(2)}) collective-permute-start(bf16[128,1024]{1,0:T(8,128)(2,1)S(1)} %copy-done.84), channel_id=1, source_target_pairs={{0,1},{1,2},{2,3},{3,0},{4,5},{5,6},{6,7},{7,4},{8,9},{9,10},{10,1... | collective-permute-start | bytes 786440 | tf_op jit(solution)/shard_map/ppermute | solution.py:176
  87.8 23.7 %collective-permute-start.24 = (bf16[128,1024]{0,1:T(8,128)(2,1)S(1)}, bf16[128,1024]{0,1:T(8,128)(2,1)S(1)}, u32[]{:S(2)}, u32[]{:S(2)}) collective-permute-start(bf16[128,1024]{0,1:T(8,128)(2,1)S(1)} %bitcast.135), channel_id=1, source_target_pairs={{0,2},{1,3},{2,0},{3,1},{4,6},{5,7},{6,4},{7,5},{8,10},{9,11},{10,... | collective-permute-start | bytes 786440 | tf_op jit(solution)/shard_map/ppermute | solution.py:176
  91.0 23.0 %collective-permute-start.25 = (bf16[128,1024]{0,1:T(8,128)(2,1)S(1)}, bf16[128,1024]{0,1:T(8,128)(2,1)S(1)}, u32[]{:S(2)}, u32[]{:S(2)}) collective-permute-start(bf16[128,1024]{0,1:T(8,128)(2,1)S(1)} %bitcast.136), channel_id=1, source_target_pairs={{0,3},{1,0},{2,1},{3,2},{4,7},{5,4},{6,5},{7,6},{8,11},{9,8},{10,9... | collective-permute-start | bytes 786440 | tf_op jit(solution)/shard_map/ppermute | solution.py:176
  116.6 30.1 %collective-permute-start.17 = (bf16[128,2048]{1,0:T(8,128)(2,1)S(1)}, bf16[128,2048]{1,0:T(8,128)(2,1)S(1)}, u32[]{:S(2)}, u32[]{:S(2)}) collective-permute-start(bf16[128,2048]{1,0:T(8,128)(2,1)S(1)} %constant_dynamic-update-slice_fusion.49), channel_id=1, source_target_pairs={{0,16},{4,20},{8,24},{12,28},{16,0},{20,4},{24,8},{28,12},{1,17},{... | collective-permute-start | bytes 1572872 | tf_op jit(solution)/shard_map/ppermute | solution.py:173
  117.2 31.5 %collective-permute-start.16 = (bf16[128,2048]{1,0:T(8,128)(2,1)S(1)}, bf16[128,2048]{1,0:T(8,128)(2,1)S(1)}, u32[]{:S(2)}, u32[]{:S(2)}) collective-permute-start(bf16[128,2048]{1,0:T(8,128)(2,1)S(1)} %constant_dynamic-update-slice_fusion.49), channel_id=1, source_target_pairs={{0,8},{4,12},{8,0},{12,4},{16,24},{20,28},{24,16},{28,20},{1,9},{5... | collective-permute-start | bytes 1572872 | tf_op jit(solution)/shard_map/ppermute | solution.py:173
  120.7 27.4 %collective-permute-start.11 = (bf16[128,2048]{1,0:T(8,128)(2,1)S(1)}, bf16[128,2048]{1,0:T(8,128)(2,1)S(1)}, u32[]{:S(2)}, u32[]{:S(2)}) collective-permute-start(bf16[128,2048]{1,0:T(8,128)(2,1)S(1)} %constant_dynamic-update-slice_fusion.47), channel_id=1, source_target_pairs={{0,8},{4,12},{8,0},{12,4},{16,24},{20,28},{24,16},{28,20},{1,9},{5... | collective-permute-start | bytes 1572872 | tf_op jit(solution)/shard_map/ppermute | solution.py:173
  122.2 22.3 %collective-permute-start.8 = (bf16[128,1024]{0,1:T(8,128)(2,1)S(1)}, bf16[128,1024]{0,1:T(8,128)(2,1)S(1)}, u32[]{:S(2)}, u32[]{:S(2)}) collective-permute-start(bf16[128,1024]{0,1:T(8,128)(2,1)S(1)} %collective-permute-done.7), channel_id=1, source_target_pairs={{0,8},{4,12},{8,0},{12,4},{16,24},{20,28},{24,16},{28,20},{1,9},{5... | collective-permute-start | bytes 786440 | tf_op jit(solution)/shard_map/ppermute | solution.py:173
  124.2 21.8 %collective-permute-start.3 = (bf16[128,1024]{0,1:T(8,128)(2,1)S(1)}, bf16[128,1024]{0,1:T(8,128)(2,1)S(1)}, u32[]{:S(2)}, u32[]{:S(2)}) collective-permute-start(bf16[128,1024]{0,1:T(8,128)(2,1)S(1)} %collective-permute-done.1), channel_id=1, source_target_pairs={{0,16},{4,20},{8,24},{12,28},{16,0},{20,4},{24,8},{28,12},{1,17},{... | collective-permute-start | bytes 786440 | tf_op jit(solution)/shard_map/ppermute | solution.py:173
  146.1 22.1 %collective-permute-start.27 = (bf16[128,2048]{0,1:T(8,128)(2,1)S(1)}, bf16[128,2048]{0,1:T(8,128)(2,1)S(1)}, u32[]{:S(2)}, u32[]{:S(2)}) collective-permute-start(bf16[128,2048]{0,1:T(8,128)(2,1)S(1)} %constant_dynamic-update-slice_fusion.51), channel_id=1, source_target_pairs={{0,16},{4,20},{8,24},{12,28},{16,0},{20,4},{24,8},{28,12},{1,17},{... | collective-permute-start | bytes 1572872 | tf_op jit(solution)/shard_map/ppermute | solution.py:173
  146.7 23.1 %collective-permute-start.21 = (bf16[128,2048]{0,1:T(8,128)(2,1)S(1)}, bf16[128,2048]{0,1:T(8,128)(2,1)S(1)}, u32[]{:S(2)}, u32[]{:S(2)}) collective-permute-start(bf16[128,2048]{0,1:T(8,128)(2,1)S(1)} %pad_maximum_fusion.6), channel_id=1, source_target_pairs={{0,8},{4,12},{8,0},{12,4},{16,24},{20,28},{24,16},{28,20},{1,9},{5... | collective-permute-start | bytes 1572872 | tf_op jit(solution)/shard_map/ppermute | solution.py:173
  148.1 22.5 %collective-permute-start.18 = (bf16[128,2048]{1,0:T(8,128)(2,1)S(1)}, bf16[128,2048]{1,0:T(8,128)(2,1)S(1)}, u32[]{:S(2)}, u32[]{:S(2)}) collective-permute-start(bf16[128,2048]{1,0:T(8,128)(2,1)S(1)} %collective-permute-done.17), channel_id=1, source_target_pairs={{0,8},{4,12},{8,0},{12,4},{16,24},{20,28},{24,16},{28,20},{1,9},{5... | collective-permute-start | bytes 1572872 | tf_op jit(solution)/shard_map/ppermute | solution.py:173
  148.7 29.1 %collective-permute-start.13 = (bf16[128,2048]{1,0:T(8,128)(2,1)S(1)}, bf16[128,2048]{1,0:T(8,128)(2,1)S(1)}, u32[]{:S(2)}, u32[]{:S(2)}) collective-permute-start(bf16[128,2048]{1,0:T(8,128)(2,1)S(1)} %collective-permute-done.11), channel_id=1, source_target_pairs={{0,16},{4,20},{8,24},{12,28},{16,0},{20,4},{24,8},{28,12},{1,17},{... | collective-permute-start | bytes 1572872 | tf_op jit(solution)/shard_map/ppermute | solution.py:173
  159.3 52.6 %collective-permute-start.9 = (bf16[512,2048]{0,1:T(8,128)(2,1)S(1)}, bf16[512,2048]{0,1:T(8,128)(2,1)S(1)}, u32[]{:S(2)}, u32[]{:S(2)}) collective-permute-start(bf16[512,2048]{0,1:T(8,128)(2,1)S(1)} %maximum_maximum_fusion.2), channel_id=1, source_target_pairs={{0,4},{4,0},{8,12},{12,8},{16,20},{20,16},{24,28},{28,24},{1,5},{5... | collective-permute-start | bytes 6291464 | tf_op jit(solution)/shard_map/ppermute | solution.py:173
  168.2 26.6 %collective-permute-start.26 = (bf16[128,2048]{0,1:T(8,128)(2,1)S(1)}, bf16[128,2048]{0,1:T(8,128)(2,1)S(1)}, u32[]{:S(2)}, u32[]{:S(2)}) collective-permute-start(bf16[128,2048]{0,1:T(8,128)(2,1)S(1)} %constant_dynamic-update-slice_fusion.51), channel_id=1, source_target_pairs={{0,8},{4,12},{8,0},{12,4},{16,24},{20,28},{24,16},{28,20},{1,9},{5... | collective-permute-start | bytes 1572872 | tf_op jit(solution)/shard_map/ppermute | solution.py:173
  169.7 25.2 %collective-permute-start.22 = (bf16[128,2048]{0,1:T(8,128)(2,1)S(1)}, bf16[128,2048]{0,1:T(8,128)(2,1)S(1)}, u32[]{:S(2)}, u32[]{:S(2)}) collective-permute-start(bf16[128,2048]{0,1:T(8,128)(2,1)S(1)} %pad_maximum_fusion.6), channel_id=1, source_target_pairs={{0,16},{4,20},{8,24},{12,28},{16,0},{20,4},{24,8},{28,12},{1,17},{... | collective-permute-start | bytes 1572872 | tf_op jit(solution)/shard_map/ppermute | solution.py:173
  170.6 24.3 %collective-permute-start.28 = (bf16[128,2048]{0,1:T(8,128)(2,1)S(1)}, bf16[128,2048]{0,1:T(8,128)(2,1)S(1)}, u32[]{:S(2)}, u32[]{:S(2)}) collective-permute-start(bf16[128,2048]{0,1:T(8,128)(2,1)S(1)} %collective-permute-done.27), channel_id=1, source_target_pairs={{0,8},{4,12},{8,0},{12,4},{16,24},{20,28},{24,16},{28,20},{1,9},{5... | collective-permute-start | bytes 1572872 | tf_op jit(solution)/shard_map/ppermute | solution.py:173
  194.9 47.8 %collective-permute-start.19 = (bf16[512,4096]{1,0:T(8,128)(2,1)}, bf16[512,4096]{1,0:T(8,128)(2,1)}, u32[]{:S(2)}, u32[]{:S(2)}) collective-permute-start(bf16[512,4096]{1,0:T(8,128)(2,1)} %maximum_maximum_fusion), channel_id=1, source_target_pairs={{0,4},{4,0},{8,12},{12,8},{16,20},{20,16},{24,28},{28,24},{1,5},{5... | collective-permute-start | bytes 12582920 | tf_op jit(solution)/shard_map/ppermute | solution.py:173
  211.8 44.0 %collective-permute-start.29 = (bf16[512,4096]{0,1:T(8,128)(2,1)}, bf16[512,4096]{0,1:T(8,128)(2,1)}, u32[]{:S(2)}, u32[]{:S(2)}) collective-permute-start(bf16[512,4096]{0,1:T(8,128)(2,1)} %maximum_maximum_fusion.1), channel_id=1, source_target_pairs={{0,4},{4,0},{8,12},{12,8},{16,20},{20,16},{24,28},{28,24},{1,5},{5... | collective-permute-start | bytes 12582920 | tf_op jit(solution)/shard_map/ppermute | solution.py:173
  331.5 173.8 %collective-permute-start.67 = (bf16[512,4096]{1,0:T(8,128)(2,1)}, bf16[512,4096]{1,0:T(8,128)(2,1)}, u32[]{:S(2)}, u32[]{:S(2)}) collective-permute-start(bf16[512,4096]{1,0:T(8,128)(2,1)} %convolution_convert_fusion), channel_id=1, source_target_pairs={{0,4},{4,0},{8,12},{12,8},{16,20},{20,16},{24,28},{28,24},{1,5},{5... | collective-permute-start | bytes 12582920 | tf_op jit(solution)/shard_map/ppermute | solution.py:173
  345.3 120.1 %collective-permute-start.47 = (bf16[512,2048]{0,1:T(8,128)(2,1)}, bf16[512,2048]{0,1:T(8,128)(2,1)}, u32[]{:S(2)}, u32[]{:S(2)}) collective-permute-start(bf16[512,2048]{0,1:T(8,128)(2,1)} %bitcast.51), channel_id=1, source_target_pairs={{0,4},{4,0},{8,12},{12,8},{16,20},{20,16},{24,28},{28,24},{1,5},{5... | collective-permute-start | bytes 6291464 | tf_op jit(solution)/shard_map/ppermute | solution.py:173
  360.5 29.6 %collective-permute-start.42 = (f32[11,1024]{1,0:T(8,128)S(1)}, f32[11,1024]{1,0:T(8,128)S(1)}, u32[]{:S(2)}, u32[]{:S(2)}) collective-permute-start(f32[11,1024]{1,0:T(8,128)S(1)} %constant_dynamic-update-slice_fusion.81), channel_id=1, source_target_pairs={{0,4},{4,0},{8,12},{12,8},{16,20},{20,16},{24,28},{28,24},{1,5},{5... | collective-permute-start | bytes 135176 | tf_op jit(solution)/shard_map/ppermute | solution.py:173
  379.0 28.0 %collective-permute-start.30 = (bf16[384,256]{1,0:T(8,128)(2,1)}, bf16[384,256]{1,0:T(8,128)(2,1)}, u32[]{:S(2)}, u32[]{:S(2)}) collective-permute-start(bf16[384,256]{1,0:T(8,128)(2,1)} %get-tuple-element.145), channel_id=1, source_target_pairs={{0,1},{1,2},{2,3},{3,0},{4,5},{5,6},{6,7},{7,4},{8,9},{9,10},{10,1... | collective-permute-start | bytes 589832 | tf_op jit(solution)/shard_map/ppermute | solution.py:176
  407.7 33.7 %collective-permute-start.36 = (bf16[384,1024]{1,0:T(8,128)(2,1)S(1)}, bf16[384,1024]{1,0:T(8,128)(2,1)S(1)}, u32[]{:S(2)}, u32[]{:S(2)}) collective-permute-start(bf16[384,1024]{1,0:T(8,128)(2,1)S(1)} %copy-done.55), channel_id=1, source_target_pairs={{0,1},{1,2},{2,3},{4,5},{5,6},{6,7},{8,9},{9,10},{10,11},{12,13},{... | collective-permute-start | bytes 2359304 | tf_op jit(solution)/shard_map/ppermute | solution.py:397
  413.9 30.3 %collective-permute-start.37 = (bf16[384,1024]{1,0:T(8,128)(2,1)S(1)}, bf16[384,1024]{1,0:T(8,128)(2,1)S(1)}, u32[]{:S(2)}, u32[]{:S(2)}) collective-permute-start(bf16[384,1024]{1,0:T(8,128)(2,1)S(1)} %copy-done.55), channel_id=1, source_target_pairs={{1,0},{2,1},{3,2},{5,4},{6,5},{7,6},{9,8},{10,9},{11,10},{13,12},{... | collective-permute-start | bytes 2359304 | tf_op jit(solution)/shard_map/ppermute | solution.py:398
  415.2 24.0 %collective-permute-start.46 = (f32[11,1024]{1,0:T(8,128)S(1)}, f32[11,1024]{1,0:T(8,128)S(1)}, u32[]{:S(2)}, u32[]{:S(2)}) collective-permute-start(f32[11,1024]{1,0:T(8,128)S(1)} %add.666), channel_id=1, source_target_pairs={{0,2},{1,3},{2,0},{3,1},{4,6},{5,7},{6,4},{7,5},{8,10},{9,11},{10,... | collective-permute-start | bytes 135176 | tf_op jit(solution)/shard_map/ppermute | solution.py:179
  439.3 72.2 %collective-permute-start.57 = (bf16[512,4096]{1,0:T(8,128)(2,1)S(1)}, bf16[512,4096]{1,0:T(8,128)(2,1)S(1)}, u32[]{:S(2)}, u32[]{:S(2)}) collective-permute-start(bf16[512,4096]{1,0:T(8,128)(2,1)S(1)} %copy-done.13), channel_id=1, source_target_pairs={{0,4},{4,0},{8,12},{12,8},{16,20},{20,16},{24,28},{28,24},{1,5},{5... | collective-permute-start | bytes 12582920 | tf_op jit(solution)/shard_map/ppermute | solution.py:173
  441.5 19.5 %collective-permute-start.38 = (bf16[384,1024]{1,0:T(8,128)(2,1)S(1)}, bf16[384,1024]{1,0:T(8,128)(2,1)S(1)}, u32[]{:S(2)}, u32[]{:S(2)}) collective-permute-start(bf16[384,1024]{1,0:T(8,128)(2,1)S(1)} %collective-permute-done.36), channel_id=1, source_target_pairs={{0,1},{1,2},{2,3},{4,5},{5,6},{6,7},{8,9},{9,10},{10,11},{12,13},{... | collective-permute-start | bytes 2359304 | tf_op jit(solution)/shard_map/ppermute | solution.py:397
  444.2 33.1 %collective-permute-start.39 = (bf16[384,1024]{1,0:T(8,128)(2,1)S(1)}, bf16[384,1024]{1,0:T(8,128)(2,1)S(1)}, u32[]{:S(2)}, u32[]{:S(2)}) collective-permute-start(bf16[384,1024]{1,0:T(8,128)(2,1)S(1)} %collective-permute-done.37), channel_id=1, source_target_pairs={{1,0},{2,1},{3,2},{5,4},{6,5},{7,6},{9,8},{10,9},{11,10},{13,12},{... | collective-permute-start | bytes 2359304 | tf_op jit(solution)/shard_map/ppermute | solution.py:398
  461.0 25.8 %collective-permute-start.40 = (bf16[384,1024]{1,0:T(8,128)(2,1)S(1)}, bf16[384,1024]{1,0:T(8,128)(2,1)S(1)}, u32[]{:S(2)}, u32[]{:S(2)}) collective-permute-start(bf16[384,1024]{1,0:T(8,128)(2,1)S(1)} %collective-permute-done.38), channel_id=1, source_target_pairs={{0,1},{1,2},{2,3},{4,5},{5,6},{6,7},{8,9},{9,10},{10,11},{12,13},{... | collective-permute-start | bytes 2359304 | tf_op jit(solution)/shard_map/ppermute | solution.py:397
  481.8 19.3 %collective-permute-start.41 = (bf16[384,1024]{1,0:T(8,128)(2,1)S(1)}, bf16[384,1024]{1,0:T(8,128)(2,1)S(1)}, u32[]{:S(2)}, u32[]{:S(2)}) collective-permute-start(bf16[384,1024]{1,0:T(8,128)(2,1)S(1)} %collective-permute-done.39), channel_id=1, source_target_pairs={{1,0},{2,1},{3,2},{5,4},{6,5},{7,6},{9,8},{10,9},{11,10},{13,12},{... | collective-permute-start | bytes 2359304 | tf_op jit(solution)/shard_map/ppermute | solution.py:398
  504.0 20.2 %collective-permute-start.51 = (bf16[128,512]{0,1:T(8,128)(2,1)S(1)}, bf16[128,512]{0,1:T(8,128)(2,1)S(1)}, u32[]{:S(2)}, u32[]{:S(2)}) collective-permute-start(bf16[128,512]{0,1:T(8,128)(2,1)S(1)} %slice.418), channel_id=1, source_target_pairs={{0,3},{1,0},{2,1},{3,2},{4,7},{5,4},{6,5},{7,6},{8,11},{9,8},{10,9... | collective-permute-start | bytes 393224 | tf_op jit(solution)/shard_map/ppermute | solution.py:176
  511.4 34.2 %collective-permute-start.68 = (bf16[128,2048]{1,0:T(8,128)(2,1)S(1)}, bf16[128,2048]{1,0:T(8,128)(2,1)S(1)}, u32[]{:S(2)}, u32[]{:S(2)}) collective-permute-start(bf16[128,2048]{1,0:T(8,128)(2,1)S(1)} %get-tuple-element.119), channel_id=1, source_target_pairs={{0,16},{4,20},{8,24},{12,28},{16,0},{20,4},{24,8},{28,12},{1,17},{... | collective-permute-start | bytes 1572872 | tf_op jit(solution)/shard_map/ppermute | solution.py:173
  521.7 22.5 %collective-permute-start.59 = (bf16[128,2048]{1,0:T(8,128)(2,1)S(1)}, bf16[128,2048]{1,0:T(8,128)(2,1)S(1)}, u32[]{:S(2)}, u32[]{:S(2)}) collective-permute-start(bf16[128,2048]{1,0:T(8,128)(2,1)S(1)} %get-tuple-element.125), channel_id=1, source_target_pairs={{0,16},{4,20},{8,24},{12,28},{16,0},{20,4},{24,8},{28,12},{1,17},{... | collective-permute-start | bytes 1572872 | tf_op jit(solution)/shard_map/ppermute | solution.py:173
  524.2 21.5 %collective-permute-start.70 = (bf16[128,2048]{1,0:T(8,128)(2,1)S(1)}, bf16[128,2048]{1,0:T(8,128)(2,1)S(1)}, u32[]{:S(2)}, u32[]{:S(2)}) collective-permute-start(bf16[128,2048]{1,0:T(8,128)(2,1)S(1)} %add_convert_fusion.13), channel_id=1, source_target_pairs={{0,8},{4,12},{8,0},{12,4},{16,24},{20,28},{24,16},{28,20},{1,9},{5... | collective-permute-start | bytes 1572872 | tf_op jit(solution)/shard_map/ppermute | solution.py:173
  525.8 26.0 %collective-permute-start.58 = (bf16[128,2048]{1,0:T(8,128)(2,1)S(1)}, bf16[128,2048]{1,0:T(8,128)(2,1)S(1)}, u32[]{:S(2)}, u32[]{:S(2)}) collective-permute-start(bf16[128,2048]{1,0:T(8,128)(2,1)S(1)} %get-tuple-element.124), channel_id=1, source_target_pairs={{0,16},{4,20},{8,24},{12,28},{16,0},{20,4},{24,8},{28,12},{1,17},{... | collective-permute-start | bytes 1572872 | tf_op jit(solution)/shard_map/ppermute | solution.py:173
  548.5 21.9 %collective-permute-start.73 = (bf16[128,2048]{1,0:T(8,128)(2,1)S(1)}, bf16[128,2048]{1,0:T(8,128)(2,1)S(1)}, u32[]{:S(2)}, u32[]{:S(2)}) collective-permute-start(bf16[128,2048]{1,0:T(8,128)(2,1)S(1)} %get-tuple-element.117), channel_id=1, source_target_pairs={{0,8},{4,12},{8,0},{12,4},{16,24},{20,28},{24,16},{28,20},{1,9},{5... | collective-permute-start | bytes 1572872 | tf_op jit(solution)/shard_map/ppermute | solution.py:173
  549.4 45.3 %collective-permute-start.72 = (bf16[128,2048]{1,0:T(8,128)(2,1)}, bf16[128,2048]{1,0:T(8,128)(2,1)S(1)}, u32[]{:S(2)}, u32[]{:S(2)}) collective-permute-start(bf16[128,2048]{1,0:T(8,128)(2,1)} %get-tuple-element.118), channel_id=1, source_target_pairs={{0,8},{4,12},{8,0},{12,4},{16,24},{20,28},{24,16},{28,20},{1,9},{5... | collective-permute-start | bytes 1572872 | tf_op jit(solution)/shard_map/ppermute | solution.py:173
  561.0 29.6 %collective-permute-start.63 = (bf16[128,2048]{1,0:T(8,128)(2,1)}, bf16[128,2048]{1,0:T(8,128)(2,1)}, u32[]{:S(2)}, u32[]{:S(2)}) collective-permute-start(bf16[128,2048]{1,0:T(8,128)(2,1)} %get-tuple-element.122), channel_id=1, source_target_pairs={{0,8},{4,12},{8,0},{12,4},{16,24},{20,28},{24,16},{28,20},{1,9},{5... | collective-permute-start | bytes 1572872 | tf_op jit(solution)/shard_map/ppermute | solution.py:173
  572.6 22.8 %collective-permute-start.74 = (bf16[128,2048]{1,0:T(8,128)(2,1)}, bf16[128,2048]{1,0:T(8,128)(2,1)S(1)}, u32[]{:S(2)}, u32[]{:S(2)}) collective-permute-start(bf16[128,2048]{1,0:T(8,128)(2,1)} %add_convert_fusion.6), channel_id=1, source_target_pairs={{0,16},{4,20},{8,24},{12,28},{16,0},{20,4},{24,8},{28,12},{1,17},{... | collective-permute-start | bytes 1572872 | tf_op jit(solution)/shard_map/ppermute | solution.py:173
  576.6 29.0 %collective-permute-start.71 = (bf16[128,1024]{1,0:T(8,128)(2,1)S(1)}, bf16[128,1024]{1,0:T(8,128)(2,1)S(1)}, u32[]{:S(2)}, u32[]{:S(2)}) collective-permute-start(bf16[128,1024]{1,0:T(8,128)(2,1)S(1)} %slice.464), channel_id=1, source_target_pairs={{0,3},{1,0},{2,1},{3,2},{4,7},{5,4},{6,5},{7,6},{8,11},{9,8},{10,9... | collective-permute-start | bytes 786440 | tf_op jit(solution)/shard_map/ppermute | solution.py:176
  590.6 31.3 %collective-permute-start.61 = (bf16[128,1024]{1,0:T(8,128)(2,1)S(1)}, bf16[128,1024]{1,0:T(8,128)(2,1)}, u32[]{:S(2)}, u32[]{:S(2)}) collective-permute-start(bf16[128,1024]{1,0:T(8,128)(2,1)S(1)} %slice.444), channel_id=1, source_target_pairs={{0,3},{1,0},{2,1},{3,2},{4,7},{5,4},{6,5},{7,6},{8,11},{9,8},{10,9... | collective-permute-start | bytes 786440 | tf_op jit(solution)/shard_map/ppermute | solution.py:176
  597.0 23.8 %collective-permute-start.75 = (bf16[128,1024]{1,0:T(8,128)(2,1)S(1)}, bf16[128,1024]{1,0:T(8,128)(2,1)S(1)}, u32[]{:S(2)}, u32[]{:S(2)}) collective-permute-start(bf16[128,1024]{1,0:T(8,128)(2,1)S(1)} %get-tuple-element.146), channel_id=1, source_target_pairs={{0,2},{1,3},{2,0},{3,1},{4,6},{5,7},{6,4},{7,5},{8,10},{9,11},{10,... | collective-permute-start | bytes 786440 | tf_op jit(solution)/shard_map/ppermute | solution.py:176
  597.1 23.7 %collective-permute-start.76 = (bf16[128,1024]{1,0:T(8,128)(2,1)S(1)}, bf16[128,1024]{1,0:T(8,128)(2,1)S(1)}, u32[]{:S(2)}, u32[]{:S(2)}) collective-permute-start(bf16[128,1024]{1,0:T(8,128)(2,1)S(1)} %get-tuple-element.147), channel_id=1, source_target_pairs={{0,1},{1,2},{2,3},{3,0},{4,5},{5,6},{6,7},{7,4},{8,9},{9,10},{10,1... | collective-permute-start | bytes 786440 | tf_op jit(solution)/shard_map/ppermute | solution.py:176
  (137 other events, 2288.3 us)
